TPU v7x, 32 devices: a whole 2x2x4 slice. The times are simulated.
32 devices in a mesh: space: 4 (over y, core), vel: 8 (over z, x).
Axes of the slice: x: 2, y: 2, z: 4, core: 2. Of those that a mesh axis runs over, the one named last changes fastest.
Arguments:
- distribution: float32 [4, 256, 13824], P('space', None, 'vel'), may hold values from -6 to 6
- neighbours: int32 [4, 4], P('space'), may hold values from -1 to 3, as said below
- block_level: int32 [4], P('space'), may hold values from 0 to 2
- collide_mask: int32 [1024], P('space'), may hold values from 0 to 1, as said below
- gain_first: float32 [6, 13824], replicated, may hold values from -1.8 to 1.8
- gain_second: float32 [6, 13824], replicated, may hold values from -1.8 to 1.8
- loss_rates: float32 [13824], replicated, may hold values from 0.2 to 2
Outputs:
- distribution_next: float32 [4, 256, 13824], P('space', None, 'vel')
Inputs may be any that keep to these rules, and one draw needn't show every extreme that they name: `neighbours`: each entry is -1 or a block held by the same index of space as the block itself or by the index one below or one above (index s holds blocks s * 1 to (s + 1) - 1). `collide_mask`: the cells of one index of space (its 1 block) hold at most 128 ones, and some index holds exactly 128.
All inputs are finite; a program needn't handle non-finite values.
Results may differ from a plain program's by a relative error of at most 0.0003.
Values sent between devices are 32-bit elements; how exact they have to be, the bound alone decides.
A program may use at most 128 MiB of HBM per device.

v0:
```python
import jax
import jax.numpy as jnp
from jax import lax
from jax.sharding import PartitionSpec as P

BSIDE = 16
VDIM = 24
ACT = 128


weno_eps = 1e-06
courant = 0.2


def extended(cells, sides, width):
    for axis, dim in sides:
        count = lax.axis_size(axis)
        ends = count - 1
        head = lax.slice_in_dim(cells, 0, width, axis=dim)
        tail = lax.slice_in_dim(cells, cells.shape[dim] - width, cells.shape[dim], axis=dim)
        cells = jnp.concatenate(
            [
                lax.ppermute(tail, axis, [(i, (i + 1) % count) for i in range(ends)]),
                cells,
                lax.ppermute(head, axis, [((i + 1) % count, i) for i in range(ends)]),
            ],
            axis=dim,
        )
    return cells


def weno_value(minus_two, minus_one, middle, plus_one, plus_two):
    guess_low = (2.0 * minus_two - 7.0 * minus_one + 11.0 * middle) / 6.0
    guess_mid = (-minus_one + 5.0 * middle + 2.0 * plus_one) / 6.0
    guess_high = (2.0 * middle + 5.0 * plus_one - plus_two) / 6.0
    rough_low = (
        13.0 / 12.0 * (minus_two - 2.0 * minus_one + middle) ** 2
        + 0.25 * (minus_two - 4.0 * minus_one + 3.0 * middle) ** 2
    )
    rough_mid = (
        13.0 / 12.0 * (minus_one - 2.0 * middle + plus_one) ** 2
        + 0.25 * (minus_one - plus_one) ** 2
    )
    rough_high = (
        13.0 / 12.0 * (middle - 2.0 * plus_one + plus_two) ** 2
        + 0.25 * (3.0 * middle - 4.0 * plus_one + plus_two) ** 2
    )
    weight_low = 0.1 / (weno_eps + rough_low) ** 2
    weight_mid = 0.6 / (weno_eps + rough_mid) ** 2
    weight_high = 0.3 / (weno_eps + rough_high) ** 2
    return (weight_low * guess_low + weight_mid * guess_mid + weight_high * guess_high) / (
        weight_low + weight_mid + weight_high
    )


def edge_values(padded, along, cell_count):

    def shifted(offset):
        return lax.slice_in_dim(padded, offset, offset + cell_count + 1, axis=along)

    upwind_low = weno_value(shifted(0), shifted(1), shifted(2), shifted(3), shifted(4))
    upwind_high = weno_value(shifted(5), shifted(4), shifted(3), shifted(2), shifted(1))
    return (upwind_low, upwind_high)


def flux_change(padded, along, cell_count, velocity):
    from_low, from_high = edge_values(padded, along, cell_count)
    step_low = lax.slice_in_dim(from_low, 1, cell_count + 1, axis=along) - lax.slice_in_dim(
        from_low, 0, cell_count, axis=along
    )
    step_high = lax.slice_in_dim(from_high, 1, cell_count + 1, axis=along) - lax.slice_in_dim(
        from_high, 0, cell_count, axis=along
    )
    return jnp.maximum(velocity, 0.0) * step_low + jnp.minimum(velocity, 0.0) * step_high


def transport_rate(
    padded_first, padded_second, along, cell_count, speed_first, speed_second, courant_ratio
):
    change = flux_change(padded_first, along, cell_count, speed_first) + flux_change(
        padded_second, along + 1, cell_count, speed_second
    )
    return -courant_ratio * change


def grid_speeds(vel_start, vel_width, vdim):
    index = vel_start + jnp.arange(vel_width, dtype=jnp.int32)
    first_index = index // (vdim * vdim)
    second_index = index // vdim % vdim
    half = (vdim - 1) / 2.0
    return (
        (first_index.astype(jnp.float32) - half) / half,
        (second_index.astype(jnp.float32) - half) / half,
    )


def hartley(length):
    grid_index = jnp.arange(length, dtype=jnp.float32)
    angle_table = 2.0 * jnp.pi * grid_index[:, None] * grid_index[None, :] / length
    return (jnp.cos(angle_table) + jnp.sin(angle_table)) / jnp.sqrt(jnp.float32(length))


def hartley_cube(velocity_cube, hartley_table):
    highest = lax.Precision.HIGHEST
    row_count, vdim = (velocity_cube.shape[0], hartley_table.shape[0])
    current = velocity_cube
    for turn in range(3):
        mapped = jnp.dot(
            current.reshape(-1, vdim),
            hartley_table,
            precision=highest,
            preferred_element_type=jnp.float32,
        )
        current = jnp.transpose(mapped.reshape(row_count, vdim, vdim, vdim), (0, 3, 1, 2))
    return current


def collide(cell_rows, gain_first, gain_second, loss_rates, hartley_table):
    row_count = cell_rows.shape[0]
    vdim = hartley_table.shape[0]
    terms = gain_first.shape[0]
    velocity_cube = cell_rows.reshape(row_count, vdim, vdim, vdim)
    spectrum = hartley_cube(velocity_cube, hartley_table)
    multipliers = jnp.concatenate([gain_first, gain_second, loss_rates[None]], axis=0).reshape(
        -1, 1, vdim, vdim, vdim
    )
    stacked = (spectrum[None] * multipliers).reshape(-1, vdim, vdim, vdim)
    images = hartley_cube(stacked, hartley_table).reshape(
        2 * terms + 1, row_count, vdim, vdim, vdim
    )
    gain_total = jnp.sum(images[:terms] * images[terms : 2 * terms], axis=0)
    loss_part = images[2 * terms]
    return (gain_total - velocity_cube * loss_part).reshape(row_count, -1)


def shards(
    distribution, neighbours, block_level, collide_mask, gain_first, gain_second, loss_rates
):
    blocks, cell_count, vel_width = distribution.shape
    block_side = BSIDE
    density = distribution.reshape(blocks, block_side, block_side, vel_width)
    vel_start = lax.axis_index("vel") * vel_width
    speed_first, speed_second = grid_speeds(vel_start, vel_width, VDIM)
    courant_ratio = (courant * jnp.exp2(block_level.astype(jnp.float32)))[:, None, None, None]
    pool_start = (lax.axis_index("space") - 1) * blocks
    present = (neighbours >= 0).astype(jnp.float32)
    pool_index = jnp.where(neighbours >= 0, neighbours - pool_start, blocks)

    def local_rate(current):
        strip_size = 3 * block_side * vel_width
        packed = jnp.concatenate(
            [
                current[:, :3].reshape(blocks, -1),
                current[:, block_side - 3 :].reshape(blocks, -1),
                current[:, :, :3].reshape(blocks, -1),
                current[:, :, block_side - 3 :].reshape(blocks, -1),
            ],
            axis=1,
        )
        ghost_pool = extended(packed, (("space", 0),), blocks)

        def select_face(face_index, strip_index):
            strips = ghost_pool[:, strip_index * strip_size : (strip_index + 1) * strip_size]
            return strips[pool_index[:, face_index]] * present[:, face_index][:, None]

        ghost_west = select_face(0, 1).reshape(blocks, 3, block_side, vel_width)
        ghost_east = select_face(1, 0).reshape(blocks, 3, block_side, vel_width)
        ghost_south = select_face(2, 3).reshape(blocks, block_side, 3, vel_width)
        ghost_north = select_face(3, 2).reshape(blocks, block_side, 3, vel_width)
        padded_first = jnp.concatenate([ghost_west, current, ghost_east], axis=1)
        padded_second = jnp.concatenate([ghost_south, current, ghost_north], axis=2)
        return transport_rate(
            padded_first, padded_second, 1, block_side, speed_first, speed_second, courant_ratio
        )

    section_one = density + local_rate(density)
    section_two = 0.5 * density + 0.5 * (section_one + local_rate(section_one))
    hartley_table = hartley(VDIM)
    flat_cells = section_two.reshape(blocks * cell_count, vel_width)
    vel_parts = lax.axis_size("vel")
    capacity = ACT
    chosen = jnp.nonzero(collide_mask, size=capacity, fill_value=0)[0]
    filled = (jnp.arange(capacity) < jnp.sum(collide_mask)).astype(jnp.float32)
    slot_rows = flat_cells[chosen] * filled[:, None]
    collided = collide(
        lax.all_to_all(
            slot_rows.reshape(vel_parts, -1, vel_width),
            "vel",
            split_axis=0,
            concat_axis=2,
            tiled=True,
        )[0],
        gain_first,
        gain_second,
        loss_rates,
        hartley_table,
    )
    change = lax.all_to_all(collided[None], "vel", split_axis=2, concat_axis=0, tiled=True)
    change = change.reshape(capacity, vel_width) * filled[:, None]
    result = flat_cells.at[chosen].add(change)
    return result.reshape(blocks, cell_count, vel_width)


def solution(mesh):
    in_specs = (P("space", None, "vel"), P("space", None), P("space"), P("space"), P(), P(), P())
    out_specs = P("space", None, "vel")
    return jax.shard_map(shards, mesh=mesh, in_specs=in_specs, out_specs=out_specs, check_vma=False)
```

profile of v0, /device:TPU:1, one launch (start us, length us, event | category | flops | bytes accessed | tf_op | source)
XLA Modules:
  0.0 621.4 jit_solution(15037906959466052470)
XLA Ops:
  11.1 4.8 collective-permute-start
  30.4 4.8 pad_maximum_fusion
  54.4 8.4 %fusion.111 = (f32[1,16,17,1728]{3,1,2,0:T(8,128)S(1)}, f32[1,16,17,1728]{3,1,2,0:T(8,128)S(1)}) fusion(f32[1,16,19,1728]{3,1,2,0:T(8,128)S(1)} %get-tuple-element.117, f32[1,16,19,1728]{3,1,2,0:T(8,128)S(1)} %copy_dynamic-update-slice_fusion.1), kind=kLoop, calls=%fused_computation.155 | loop fusion | flops 58281984 | bytes 15040512 | tf_op jit(solution)/shard_map/div | solution.py:51
  63.1 13.3 %fusion.60 = (f32[1,17,16,1728]{3,1,2,0:T(8,128)S(1)}, f32[1,17,16,1728]{3,1,2,0:T(8,128)S(1)}) fusion(f32[1,16,16,1728]{3,1,2,0:T(8,128)S(1)} %get-tuple-element.115, f32[1,3,16,1728]{3,1,2,0:T(4,128)S(1)} %copy-done.5, f32[1,19,16,1728]{3,1,2,0:T(8,128)S(1)} %copy_dynamic-update-slice_fusion), kind=kLoop, calls=%fused_computation.89 | loop fusion | flops 60162048 | bytes 11501568 | tf_op jit(solution)/shard_map/div | solution.py:51
  100.5 8.2 %collective-permute-done.3 = f32[1,331776]{1,0:T(1,128)} collective-permute-done((f32[1,331776]{1,0:T(1,128)S(1)}, f32[1,331776]{1,0:T(1,128)}, u32[]{:S(2)}, u32[]{:S(2)}) %collective-permute-start.3) | collective-permute-done | bytes 1327136 | tf_op jit(solution)/shard_map/ppermute | solution.py:25
  109.8 5.4 pad_maximum_fusion.1
  125.4 5.3 fusion.143
  132.4 15.2 %fusion.89 = (f32[1,16,17,1728]{3,1,2,0:T(8,128)S(1)}, f32[1,16,17,1728]{3,1,2,0:T(8,128)S(1)}) fusion(f32[1,16,16,1728]{3,1,2,0:T(8,128)} %copy-done, f32[1,16,3,1728]{3,1,2,0:T(8,128)S(1)} %copy.112, f32[1,16,3,1728]{3,1,2,0:T(8,128)S(1)} %copy.113), kind=kLoop, calls=%fused_computation.128 | loop fusion | flops 63452160 | bytes 6193152 | tf_op jit(solution)/shard_map/div | solution.py:51
  147.7 13.8 %fusion.34 = (f32[1,17,16,1728]{3,1,2,0:T(8,128)S(1)}, f32[1,17,16,1728]{3,1,2,0:T(8,128)S(1)}) fusion(f32[1,16,16,1728]{3,1,2,0:T(8,128)S(1)} %copy-done.1, f32[1,3,16,1728]{3,1,2,0:T(4,128)S(1)} %copy-done.7, f32[1,3,16,1728]{3,1,2,0:T(4,128)S(1)} %copy-done.6), kind=kLoop, calls=%fused_computation.58 | loop fusion | flops 63452160 | bytes 6193152 | tf_op jit(solution)/shard_map/div | solution.py:51
  167.4 5.5 all-to-all-start
  194.0 6.0 fusion.159
  200.1 9.5 %fusion.71 = f32[16,24,24,24]{1,2,3,0:T(8,128)} fusion(f32[16,24,24,24]{3,2,1,0:T(8,128)S(1)} %fusion.159, f32[24]{0:T(128)S(1)} %iota_multiply_fusion), kind=kOutput, calls=%fused_computation.102 | convolution fusion | flops 63703296 | bytes 1769568 | tf_op jit(solution)/shard_map/dot_general | solution.py:108
  209.5 6.3 %copy.121 = f32[16,24,24,24]{3,2,1,0:T(8,128)} copy(f32[16,24,24,24]{1,2,3,0:T(8,128)} %fusion.71) | data formatting | bytes 1769472 | tf_op jit(solution)/shard_map/transpose | solution.py:114
  215.8 7.6 %convolution_bitcast_fusion = f32[16,24,24,24]{1,3,2,0:T(8,128)} fusion(f32[16,24,24,24]{3,2,1,0:T(8,128)} %copy.121, f32[24]{0:T(128)S(1)} %iota_multiply_fusion), kind=kOutput, calls=%fused_computation.103 | convolution fusion | flops 63703296 | bytes 1769568 | tf_op jit(solution)/shard_map/dot_general | solution.py:108
  223.4 6.2 copy.123
  229.6 22.1 %broadcast_multiply_fusion = f32[13,16,24,24,24]{4,3,2,1,0:T(8,128)} fusion(f32[13,24,24,24]{3,2,1,0:T(8,128)} %maximum_bitcast_fusion, f32[16,24,24,24]{3,2,1,0:T(8,128)} %copy.123), kind=kLoop, calls=%fused_computation.5 | loop fusion | flops 2875392 | bytes 13105152 | tf_op jit(solution)/shard_map/mul | solution.py:127
  251.7 110.7 %fusion.12 = f32[208,24,24,24]{0,1,3,2:T(8,128)} fusion(f32[208,24,24,24]{3,2,1,0:T(8,128)} %bitcast.86, f32[24]{0:T(128)S(1)} %iota_multiply_fusion), kind=kOutput, calls=%fused_computation.12 | convolution fusion | flops 828115200 | bytes 23003232 | tf_op jit(solution)/shard_map/dot_general | solution.py:108
  362.4 21.1 %fusion.6 = f32[208,24,24,24]{0,1,3,2:T(8,128)S(1)} fusion(f32[208,24,24,24]{0,1,3,2:T(8,128)} %fusion.12, f32[24]{0:T(128)S(1)} %iota_multiply_fusion), kind=kOutput, calls=%fused_computation.10 | convolution fusion | flops 828115200 | bytes 23003232 | tf_op jit(solution)/shard_map/dot_general | solution.py:108
  383.6 19.6 %fusion.9 = f32[208,24,24,24]{0,1,3,2:T(8,128)} fusion(f32[208,24,24,24]{0,1,3,2:T(8,128)S(1)} %fusion.6, f32[24]{0:T(128)S(1)} %iota_multiply_fusion), kind=kOutput, calls=%fused_computation.11 | convolution fusion | flops 828115200 | bytes 23003232 | tf_op jit(solution)/shard_map/dot_general | solution.py:108
  403.2 11.8 %slice_multiply_fusion = f32[96,24,24,24]{0,1,3,2:T(8,128)} fusion(f32[208,24,24,24]{0,1,3,2:T(8,128)} %fusion.9), kind=kLoop, calls=%fused_computation.13 | loop fusion | flops 1327104 | bytes 15925248 | tf_op jit(solution)/shard_map/mul | solution.py:131
  415.0 7.7 %slice.449 = f32[16,24,24,24]{0,1,3,2:T(8,128)} slice(f32[208,24,24,24]{0,1,3,2:T(8,128)} %fusion.9), slice={[192:208], [0:24], [0:24], [0:24]} | slice | bytes 1769472 | tf_op jit(solution)/shard_map/slice | solution.py:132
  422.7 9.5 %copy.129 = f32[16,24,24,24]{3,2,1,0:T(8,128)} copy(f32[16,24,24,24]{0,1,3,2:T(8,128)} %slice.449) | data formatting | bytes 1769472 | tf_op jit(solution)/shard_map/slice | solution.py:132
  432.2 5.5 squeeze.23
  437.7 23.0 %copy.127 = f32[96,24,24,24]{3,2,1,0:T(8,128)} copy(f32[96,24,24,24]{0,1,3,2:T(8,128)} %slice_multiply_fusion) | data formatting | bytes 10616832 | tf_op jit(solution)/shard_map/mul | solution.py:131
  460.7 13.0 %reduce_sum.31 = f32[16,24,24,24]{3,2,1,0:T(8,128)} reduce(f32[6,16,24,24,24]{4,3,2,1,0:T(8,128)} %bitcast.90, f32[]{:T(128)} %constant.144.clone.1), dimensions={0}, to_apply=%region_6.7 | reduce | flops 1105920 | bytes 6193156 | tf_op jit(solution)/shard_map/reduce_sum | solution.py:131
  473.8 5.4 reduce_sum.32
  481.6 13.4 %copy.130 = f32[1,16,13824]{1,0,2:T(1,128)} copy(f32[1,16,13824]{2,1,0:T(8,128)} %multiply_subtract_fusion.8) | data formatting | bytes 1769472 | tf_op jit(solution)/shard_map/sub | solution.py:133
  495.5 66.0 %reduce.36 = f32[13824,16]{1,0:T(8,128)} reduce(f32[13824,1,16]{2,1,0:T(1,128)} %bitcast.96, f32[]{:T(128)} %broadcast.820), dimensions={1}, to_apply=%bitcast.82.reduce_sub_computation | reduce | bytes 1769476
  561.5 5.8 reshape.653
  571.9 16.0 %all-to-all-done.1 = f32[8,1,27648]{2,1,0:T(1,128)S(1)} async-done(((f32[8,1,27648]{2,1,0:T(1,128)}), f32[8,1,27648]{2,1,0:T(1,128)S(1)}, u32[]{:S(2)}, u32[]{:S(2)}) %all-to-all-start.1) | async-done | bytes 884768 | tf_op jit(solution)/shard_map/all_to_all | solution.py:198
  591.8 19.7 %reshape.654 = f32[13824,1,16]{2,1,0:T(1,128)} reshape(f32[8,27648]{1,0:T(8,128)} %reduce.37) | data formatting | bytes 1769472
  611.5 4.8 copy.142
  (147 shorter events, 116.9 us)
Async XLA Ops:
  4.2 11.7 %copy-start.22 = (s32[1,4]{1,0:T(1,128)S(1)}, s32[1,4]{1,0:T(1,128)}, u32[]{:S(2)}) copy-start(s32[1,4]{1,0:T(1,128)} %param.8) | copy-start | bytes 52
  9.2 20.1 %collective-permute-start.1 = (f32[1,331776]{1,0:T(1,128)S(1)}, f32[1,331776]{1,0:T(1,128)}, u32[]{:S(2)}, u32[]{:S(2)}) collective-permute-start(f32[1,331776]{1,0:T(1,128)S(1)} %constant_dynamic-update-slice_fusion), channel_id=1, source_target_pairs={{8,0},{16,8},{24,16},{9,1},{17,9},{25,17},{10,2},{18,10},{26,18},{... | collective-permute-start | bytes 3981320 | tf_op jit(solution)/shard_map/ppermute | solution.py:25
  11.1 19.2 %collective-permute-start = (f32[1,331776]{1,0:T(1,128)S(1)}, f32[1,331776]{1,0:T(1,128)}, u32[]{:S(2)}, u32[]{:S(2)}) collective-permute-start(f32[1,331776]{1,0:T(1,128)S(1)} %constant_dynamic-update-slice_fusion), channel_id=1, source_target_pairs={{0,8},{8,16},{16,24},{1,9},{9,17},{17,25},{2,10},{10,18},{18,26},{... | collective-permute-start | bytes 3981320 | tf_op jit(solution)/shard_map/ppermute | solution.py:23
  24.7 51.7 %copy-start.10 = (f32[1728]{0:T(1024)}, f32[1728]{0:T(1024)S(1)}, u32[]{:S(2)}) copy-start(f32[1728]{0:T(1024)S(1)} %broadcast_minimum_fusion.1) | copy-start | bytes 20740
  24.7 51.7 %copy-start.12 = (f32[1728]{0:T(1024)}, f32[1728]{0:T(1024)S(1)}, u32[]{:S(2)}) copy-start(f32[1728]{0:T(1024)S(1)} %broadcast_minimum_fusion) | copy-start | bytes 20740
  24.8 51.7 %copy-start.14 = (f32[1728]{0:T(1024)}, f32[1728]{0:T(1024)S(1)}, u32[]{:S(2)}) copy-start(f32[1728]{0:T(1024)S(1)} %broadcast_maximum_fusion) | copy-start | bytes 20740
  24.8 51.6 %copy-start.16 = (f32[1728]{0:T(1024)}, f32[1728]{0:T(1024)S(1)}, u32[]{:S(2)}) copy-start(f32[1728]{0:T(1024)S(1)} %broadcast_maximum_fusion.1) | copy-start | bytes 20740
  53.0 1.2 copy-start.4
  54.4 8.8 %copy-start.5 = (f32[1,3,16,1728]{3,1,2,0:T(4,128)S(1)}, f32[1,3,16,1728]{3,1,2,0:T(4,128)}, u32[]{:S(2)}) copy-start(f32[1,3,16,1728]{3,1,2,0:T(4,128)} %copy.97) | copy-start | bytes 995332
  78.8 1.3 copy-start
  83.3 5.4 copy-start.8
  84.4 10.7 %copy-start.21 = (s32[256]{0:T(256)S(1)}, s32[256]{0:T(256)}, u32[]{:S(2)}) copy-start(s32[256]{0:T(256)} %param.10) | copy-start | bytes 3076
  88.7 20.1 %collective-permute-start.3 = (f32[1,331776]{1,0:T(1,128)S(1)}, f32[1,331776]{1,0:T(1,128)}, u32[]{:S(2)}, u32[]{:S(2)}) collective-permute-start(f32[1,331776]{1,0:T(1,128)S(1)} %constant_dynamic-update-slice_fusion.7), channel_id=1, source_target_pairs={{8,0},{16,8},{24,16},{9,1},{17,9},{25,17},{10,2},{18,10},{26,18},{... | collective-permute-start | bytes 3981320 | tf_op jit(solution)/shard_map/ppermute | solution.py:25
  90.6 19.2 %collective-permute-start.2 = (f32[1,331776]{1,0:T(1,128)S(1)}, f32[1,331776]{1,0:T(1,128)}, u32[]{:S(2)}, u32[]{:S(2)}) collective-permute-start(f32[1,331776]{1,0:T(1,128)S(1)} %constant_dynamic-update-slice_fusion.7), channel_id=1, source_target_pairs={{0,8},{8,16},{16,24},{1,9},{9,17},{17,25},{2,10},{10,18},{18,26},{... | collective-permute-start | bytes 3981320 | tf_op jit(solution)/shard_map/ppermute | solution.py:23
  100.5 14.7 %copy-start.19 = (s32[128]{0:T(128)}, s32[128]{0:T(128)S(1)}, u32[]{:S(2)}) copy-start(s32[128]{0:T(128)S(1)} %fusion.153) | copy-start | bytes 1540
  132.4 15.2 %copy-start.1 = (f32[1,16,16,1728]{3,1,2,0:T(8,128)S(1)}, f32[1,16,16,1728]{3,1,2,0:T(8,128)}, u32[]{:S(2)}) copy-start(f32[1,16,16,1728]{3,1,2,0:T(8,128)} %copy-done) | copy-start | bytes 5308420
  132.4 15.2 %copy-start.6 = (f32[1,3,16,1728]{3,1,2,0:T(4,128)S(1)}, f32[1,3,16,1728]{3,1,2,0:T(4,128)}, u32[]{:S(2)}) copy-start(f32[1,3,16,1728]{3,1,2,0:T(4,128)} %copy.111) | copy-start | bytes 995332
  132.4 15.2 %copy-start.7 = (f32[1,3,16,1728]{3,1,2,0:T(4,128)S(1)}, f32[1,3,16,1728]{3,1,2,0:T(4,128)}, u32[]{:S(2)}) copy-start(f32[1,3,16,1728]{3,1,2,0:T(4,128)} %copy.110) | copy-start | bytes 995332
  147.7 13.9 %copy-start.11 = (f32[1728]{0:T(1024)S(1)}, f32[1728]{0:T(1024)}, u32[]{:S(2)}) copy-start(f32[1728]{0:T(1024)} %copy-done.10) | copy-start | bytes 20740
  147.7 13.9 %copy-start.13 = (f32[1728]{0:T(1024)S(1)}, f32[1728]{0:T(1024)}, u32[]{:S(2)}) copy-start(f32[1728]{0:T(1024)} %copy-done.12) | copy-start | bytes 20740
  147.7 13.9 %copy-start.15 = (f32[1728]{0:T(1024)S(1)}, f32[1728]{0:T(1024)}, u32[]{:S(2)}) copy-start(f32[1728]{0:T(1024)} %copy-done.14) | copy-start | bytes 20740
  147.7 13.9 %copy-start.17 = (f32[1728]{0:T(1024)S(1)}, f32[1728]{0:T(1024)}, u32[]{:S(2)}) copy-start(f32[1728]{0:T(1024)} %copy-done.16) | copy-start | bytes 20740
  166.3 6.6 %copy-start.18 = (f32[13824]{0:T(1024)S(1)}, f32[13824]{0:T(1024)}, u32[]{:S(2)}) copy-start(f32[13824]{0:T(1024)} %param.13) | copy-start | bytes 165892
  166.4 6.8 %copy-start.9 = (f32[6,13824]{1,0:T(8,128)S(1)}, f32[6,13824]{1,0:T(8,128)}, u32[]{:S(2)}) copy-start(f32[6,13824]{1,0:T(8,128)} %param.11) | copy-start | bytes 995332
  167.4 19.5 %all-to-all-start = ((f32[8,16,1728]{2,1,0:T(8,128)}), f32[8,16,1728]{2,1,0:T(8,128)S(1)}, u32[]{:S(2)}, u32[]{:S(2)}) async-start(f32[8,16,1728]{2,1,0:T(8,128)} %broadcast_multiply_fusion.1), calls=%async_computation | async-start | bytes 1835008 | tf_op jit(solution)/shard_map/all_to_all | solution.py:186
  186.9 0.9 copy-start.2
  473.8 5.4 copy-start.3
  567.3 20.7 %all-to-all-start.1 = ((f32[8,1,27648]{2,1,0:T(1,128)}), f32[8,1,27648]{2,1,0:T(1,128)S(1)}, u32[]{:S(2)}, u32[]{:S(2)}) async-start(f32[8,1,27648]{2,1,0:T(1,128)} %reshape.653), calls=%async_computation.1 | async-start | bytes 1769472 | tf_op jit(solution)/shard_map/all_to_all | solution.py:198
  616.3 0.6 copy-start.20
where the time goes:
time: 627 us; the launch traced here: 621 us
  other arithmetic  218 us (35%)
  matrix products  175 us (28%)
  local copies, waits for them, and re-layouts  163 us (26%)
  waiting for transfers between devices  33.7 us (5%)
  starting transfers between devices  22.6 us (4%)
  between operations  8.98 us (1%)
    dot_general x6, matrix products, hartley_cube(): jnp.dot(current.reshape(-1, vdim), hartley_table, precision=highest, pref...  175 us
    unnamed x1, other arithmetic  66 us
    div x4, other arithmetic, weno_value(): (weight_low * guess_low + weight_mid * guess_mid + weight_high * guess_hi...  50.8 us
    unnamed x57, local copies, waits for them, and re-layouts  37.3 us
    mul x2, other arithmetic, collide(): stacked = (spectrum[None] * multipliers).reshape(-1, vdim, vdim, vdim)  26.4 us
    mul x1, local copies, waits for them, and re-layouts, collide(): gain_total = jnp.sum(images[:terms] * images[terms:2 * terms], axis=0)  23 us
    mul x6, other arithmetic, select_face(): return strips[pool_index[:, face_index]] * present[:, face_index][:, None]  19.2 us
    slice x2, local copies, waits for them, and re-layouts, collide(): loss_part = images[2 * terms]  17.2 us
  transfers between devices with their start and end apart: 6, of which 6 were waited for; matrix products, arithmetic and copies ran while one was open for 3% of the time, Pallas kernels for 0%

commit v1 on v0

v1 whole, which is shorter than its diff:
```python
import functools

import jax
import jax.numpy as jnp
import numpy as np
from jax import lax
from jax.experimental import pallas as pl
from jax.experimental.pallas import tpu as pltpu
from jax.sharding import PartitionSpec as P

BSIDE = 16
VDIM = 24
ACT = 128
LANES = 128
GROUP = 8


weno_eps = 1e-06
courant = 0.2


def speed_rows(vel_start, vel_width):
    index = vel_start + jnp.arange(vel_width, dtype=jnp.int32)
    half = (VDIM - 1) / 2.0
    first = ((index // (VDIM * VDIM)).astype(jnp.float32) - half) / half
    second = ((index // VDIM % VDIM).astype(jnp.float32) - half) / half
    rows = [jnp.abs(first), jnp.abs(second), jnp.where(first < 0, 1.0, 0.0), jnp.where(second < 0, 1.0, 0.0)]
    return jnp.stack(rows + [jnp.zeros_like(first)] * 4)


def pack_kernel(u_ref, pack_ref):
    side = BSIDE
    pack_ref[0 : 3 * side] = u_ref[0 : 3 * side]
    pack_ref[3 * side : 6 * side] = u_ref[(side - 3) * side :]
    for layer in range(3):
        at = (6 + layer) * side
        pack_ref[at : at + side] = u_ref[pl.ds(layer, side, stride=side), :]
        at = (9 + layer) * side
        pack_ref[at : at + side] = u_ref[pl.ds(side - 3 + layer, side, stride=side), :]


def sweep(line, against, speed, flux_ref):
    side = BSIDE

    def oriented(n):
        return jnp.where(against, line(side + 5 - n), line(n))

    values = [oriented(n) for n in range(4)]
    slopes = [values[n + 1] - values[n] for n in range(3)]
    bends = []
    for n in range(2):
        bend = slopes[n + 1] - slopes[n]
        bends.append(bend * bend * (13.0 / 3.0) + 4.0 * weno_eps)
    before = None
    for i in range(side + 1):
        values.append(oriented(i + 4))
        slopes.append(values[i + 4] - values[i + 3])
        bend = slopes[i + 3] - slopes[i + 2]
        bends.append(bend * bend * (13.0 / 3.0) + 4.0 * weno_eps)
        d0, d1, d2, d3 = slopes[i : i + 4]
        tilt_low = 3.0 * d1 - d0
        tilt_mid = d1 + d2
        tilt_high = d3 - 3.0 * d2
        rough_low = bends[i] + tilt_low * tilt_low
        rough_mid = bends[i + 1] + tilt_mid * tilt_mid
        rough_high = bends[i + 2] + tilt_high * tilt_high
        low2 = rough_low * rough_low
        mid2 = rough_mid * rough_mid
        high2 = rough_high * rough_high
        weight_low = mid2 * high2
        low3 = 3.0 * low2
        weight_mid = (low3 + low3) * high2
        weight_high = low3 * mid2
        guess_low = 5.0 * d1 - 2.0 * d0
        guess_mid = d1 + (d2 + d2)
        guess_high = 4.0 * d2 - d3
        above = weight_low * guess_low + weight_mid * guess_mid + weight_high * guess_high
        below = weight_low + weight_mid + weight_high
        edge = values[i + 2] + above / (6.0 * below)
        if before is not None:
            flux_ref[(i - 1) * side : i * side] = speed * (edge - before)
        before = edge


def stage_kernel(final, source_ref, ratio_ref, *refs):
    if final:
        base_ref, u_ref, left_ref, right_ref, speed_ref, out_ref, flux_one, flux_two, flux_turned = refs
    else:
        u_ref, left_ref, right_ref, speed_ref, out_ref, pack_ref, flux_one, flux_two, flux_turned = refs
    side = BSIDE
    lanes = u_ref.shape[1]

    def first_line(n):
        return u_ref[n * side : (n + 1) * side]

    def second_line(n):
        return u_ref[pl.ds(n, side, stride=side), :]

    def ghost(face, strip, layer, own):
        at = (3 * strip + layer) * side
        return (
            source_ref[3 * face] * left_ref[at : at + side]
            + source_ref[3 * face + 1] * own
            + source_ref[3 * face + 2] * right_ref[at : at + side]
        )

    def padded(line, faces, strips):
        ghosts = {}
        for layer in range(3):
            ghosts[layer] = ghost(faces[0], strips[0], layer, line(side - 3 + layer))
            ghosts[side + 3 + layer] = ghost(faces[1], strips[1], layer, line(layer))
        return lambda n: ghosts[n] if n in ghosts else line(n - 3)

    def spread(row):
        return jnp.broadcast_to(speed_ref[row : row + 1], (side, lanes))

    against_first = spread(2) > 0.5
    against_second = spread(3) > 0.5
    sweep(padded(first_line, (0, 1), (1, 0)), against_first, spread(0), flux_one)
    sweep(padded(second_line, (2, 3), (3, 2)), against_second, spread(1), flux_two)
    for n in range(side):
        back = side - 1 - n
        flux_turned[n * side : (n + 1) * side] = jnp.where(
            against_second, flux_two[back * side : (back + 1) * side], flux_two[n * side : (n + 1) * side]
        )
    ratio = ratio_ref[0]
    for n in range(side):
        back = side - 1 - n
        rows = slice(n * side, (n + 1) * side)
        change = jnp.where(against_first, flux_one[back * side : (back + 1) * side], flux_one[rows])
        change = change + flux_turned[pl.ds(n, side, stride=side), :]
        moved = u_ref[rows] - ratio * change
        if final:
            moved = 0.5 * base_ref[rows] + 0.5 * moved
        out_ref[rows] = moved
    if not final:
        pack_kernel(out_ref, pack_ref)


def lane_spec(rows):
    return pl.BlockSpec((rows, LANES), lambda n: (0, n))


def pack(cells):
    count, width = cells.shape
    return pl.pallas_call(
        pack_kernel,
        grid=(pl.cdiv(width, LANES),),
        in_specs=[lane_spec(count)],
        out_specs=lane_spec(12 * BSIDE),
        out_shape=jax.ShapeDtypeStruct((12 * BSIDE, width), jnp.float32),
    )(cells)


def stage(final, source, ratio, arrays):
    count, width = arrays[0].shape
    smem = pl.BlockSpec(memory_space=pltpu.SMEM)
    full = jax.ShapeDtypeStruct((count, width), jnp.float32)
    strips = jax.ShapeDtypeStruct((12 * BSIDE, width), jnp.float32)
    return pl.pallas_call(
        functools.partial(stage_kernel, final),
        grid=(pl.cdiv(width, LANES),),
        in_specs=[smem, smem] + [lane_spec(array.shape[0]) for array in arrays],
        out_specs=lane_spec(count) if final else [lane_spec(count), lane_spec(12 * BSIDE)],
        out_shape=full if final else [full, strips],
        scratch_shapes=[pltpu.VMEM((count, LANES), jnp.float32)] * 3,
    )(source, ratio, *arrays)


def exchange(strips):
    count = lax.axis_size("space")
    up = [(i, i + 1) for i in range(count - 1)]
    return lax.ppermute(strips, "space", up), lax.ppermute(strips, "space", [(j, i) for i, j in up])


def gather_kernel(chosen_ref, cells_ref, out_ref, rows_ref):
    parts, planes, each, plane = out_ref.shape

    def one(slot, carry):
        rows_ref[pl.ds(slot, 1), :] = cells_ref[pl.ds(chosen_ref[slot], 1), :]
        return carry

    lax.fori_loop(0, parts * each, one, 0, unroll=8)
    for part in range(parts):
        for n in range(planes):
            out_ref[part, n] = rows_ref[part * each : (part + 1) * each, n * plane : (n + 1) * plane]


def gather(chosen, cells, shape):
    return pl.pallas_call(
        gather_kernel,
        in_specs=[pl.BlockSpec(memory_space=pltpu.SMEM), pl.BlockSpec(memory_space=pltpu.VMEM)],
        out_specs=pl.BlockSpec(memory_space=pltpu.VMEM),
        out_shape=jax.ShapeDtypeStruct(shape, jnp.float32),
        scratch_shapes=[pltpu.VMEM((shape[0] * shape[2], cells.shape[1]), jnp.float32)],
    )(chosen, cells)


def scatter_kernel(chosen_ref, count_ref, cells_ref, change_ref, out_ref, rows_ref):
    parts, planes, each, plane = change_ref.shape
    for part in range(parts):
        for n in range(planes):
            rows_ref[part * each : (part + 1) * each, n * plane : (n + 1) * plane] = change_ref[part, n]
    out_ref[...] = cells_ref[...]

    def one(slot, carry):
        row = pl.ds(chosen_ref[slot], 1)
        out_ref[row, :] = cells_ref[row, :] + rows_ref[pl.ds(slot, 1), :]
        return carry

    lax.fori_loop(0, count_ref[0], one, 0)


def scatter(chosen, count, cells, change):
    smem = pl.BlockSpec(memory_space=pltpu.SMEM)
    vmem = pl.BlockSpec(memory_space=pltpu.VMEM)
    return pl.pallas_call(
        scatter_kernel,
        in_specs=[smem, smem, vmem, vmem],
        out_specs=vmem,
        out_shape=jax.ShapeDtypeStruct(cells.shape, jnp.float32),
        scratch_shapes=[pltpu.VMEM((change.shape[0] * change.shape[2], cells.shape[1]), jnp.float32)],
    )(chosen, count, cells, change)


def halves(table):
    high = table.astype(jnp.bfloat16)
    low = (table - high.astype(jnp.float32)).astype(jnp.bfloat16)
    return high, low


def dot3(left, right):
    def dot(a, b):
        return jnp.dot(a, b, preferred_element_type=jnp.float32)

    return dot(left[0], right[0]) + (dot(left[1], right[0]) + dot(left[0], right[1]))


def collide_kernel(cells_ref, first_ref, second_ref, loss_ref, plane_ref, line_ref, out_ref):
    depth, group, plane = cells_ref.shape
    terms = first_ref.shape[0]
    plane_table = (plane_ref[0], plane_ref[1])
    line_table = (line_ref[0], line_ref[1])

    def transform(flat):
        return dot3(line_table, halves(dot3(halves(flat), plane_table)))

    values = cells_ref[...].reshape(depth * group, plane)
    spectrum = transform(values).reshape(depth, group, plane)

    def image(multiplier):
        return transform((spectrum * multiplier[:, None, :]).reshape(depth * group, plane))

    total = -values * image(loss_ref[...])

    def one(term, total):
        return total + image(first_ref[term]) * image(second_ref[term])

    total = lax.fori_loop(0, terms, one, total)
    out_ref[...] = total.reshape(depth, group, plane)


def hartley_tables(vdim):
    index = np.arange(vdim, dtype=np.float64)
    angle = 2.0 * np.pi * np.outer(index, index) / vdim
    table = (np.cos(angle) + np.sin(angle)) / np.sqrt(vdim)

    def split(wide):
        wide = wide.astype(np.float32)
        high = wide.astype(jnp.bfloat16)
        return np.stack([high, (wide - high.astype(np.float32)).astype(jnp.bfloat16)])

    return split(np.kron(table, table)), split(np.kron(table, np.eye(GROUP)))


def collide(cells, gain_first, gain_second, loss_rates):
    depth, count, plane = cells.shape
    spare = -count % GROUP
    if spare:
        cells = jnp.pad(cells, ((0, 0), (0, spare), (0, 0)))
    terms = gain_first.shape[0]
    plane_table, line_table = hartley_tables(VDIM)
    cell_spec = pl.BlockSpec((depth, GROUP, plane), lambda n: (0, n, 0))

    def whole(shape):
        return pl.BlockSpec(shape, lambda n: (0,) * len(shape))

    multipliers = (
        gain_first.reshape(terms, depth, plane),
        gain_second.reshape(terms, depth, plane),
        loss_rates.reshape(depth, plane),
    )
    tables = (jnp.asarray(plane_table), jnp.asarray(line_table))
    result = pl.pallas_call(
        collide_kernel,
        grid=((count + spare) // GROUP,),
        in_specs=[cell_spec] + [whole(array.shape) for array in multipliers + tables],
        out_specs=cell_spec,
        out_shape=jax.ShapeDtypeStruct(cells.shape, jnp.float32),
        compiler_params=pltpu.CompilerParams(vmem_limit_bytes=56 * 1024 * 1024),
    )(cells, *multipliers, *tables)
    return result[:, :count]


def shards(
    distribution, neighbours, block_level, collide_mask, gain_first, gain_second, loss_rates
):
    blocks, cell_count, width = distribution.shape
    assert blocks == 1
    density = distribution.reshape(cell_count, width)
    speeds = speed_rows(lax.axis_index("vel") * width, width)
    ratio = courant * jnp.exp2(block_level.astype(jnp.float32))
    offset = neighbours[0] - (lax.axis_index("space") - 1)
    source = (offset[:, None] == jnp.arange(3)) & (neighbours[0] >= 0)[:, None]
    source = source.astype(jnp.float32).reshape(-1)

    section_one, strips = stage(False, source, ratio, (density, *exchange(pack(density)), speeds))
    section_two = stage(True, source, ratio, (density, section_one, *exchange(strips), speeds))

    parts = lax.axis_size("vel")
    each = ACT // parts
    cell_index = jnp.arange(cell_count)
    rank = jnp.sum(jnp.where(cell_index[:, None] < cell_index, collide_mask[:, None], 0), axis=0)
    hit = (rank[:, None] == jnp.arange(ACT)) & (collide_mask > 0)[:, None]
    chosen = jnp.sum(jnp.where(hit, cell_index[:, None], 0), axis=0)
    held = jnp.sum(collide_mask)[None]

    plane = VDIM * VDIM
    if width % plane == 0:
        planes, span = width // plane, plane
    else:
        planes, span = 1, width
    sent = gather(chosen, section_two, (parts, planes, each, span))
    got = lax.all_to_all(sent, "vel", split_axis=0, concat_axis=0, tiled=True)
    got = got.reshape(parts * planes, each, span)
    if span != plane:
        got = jnp.transpose(got, (1, 0, 2)).reshape(each, VDIM, plane).transpose(1, 0, 2)
    change = collide(got, gain_first, gain_second, loss_rates)
    if span != plane:
        change = change.transpose(1, 0, 2).reshape(each, parts, span).transpose(1, 0, 2)
    change = change.reshape(parts, planes, each, span)
    change = lax.all_to_all(change, "vel", split_axis=0, concat_axis=0, tiled=True)
    return scatter(chosen, held, section_two, change).reshape(blocks, cell_count, width)


def solution(mesh):
    in_specs = (P("space", None, "vel"), P("space", None), P("space"), P("space"), P(), P(), P())
    out_specs = P("space", None, "vel")
    return jax.shard_map(shards, mesh=mesh, in_specs=in_specs, out_specs=out_specs, check_vma=False)
```

time: 627 us -> 171 us (0.27)
  other arithmetic: 218 us -> 1.86 us
  matrix products: 175 us -> 0 us
  local copies, waits for them, and re-layouts: 163 us -> 13.3 us
  Pallas kernels: 0 us -> 76.4 us
  waiting for transfers between devices: 33.7 us -> 57.3 us
  between operations: 8.98 us -> 0.82 us
    dot_general x6 -> x0, matrix products: 175 us -> none  [hartley_cube(): jnp.dot(current.reshape(-1, vdim), hartley_table, precision=highest, pref...]
    pallas_call x0 -> x6, Pallas kernels: none -> 76.4 us  [the longest x1 34.3 us: collide(): pl.pallas_call(collide_kernel, grid=((count + spare) // GROUP,), in_specs...]
    unnamed x1 -> x0, other arithmetic: 66 us -> none
    mul x12 -> x0, other arithmetic: 58.5 us -> none  [the longest x2 26.4 us: collide(): stacked = (spectrum[None] * multipliers).reshape(-1, vdim, vdim, vdim)]
    div x4 -> x0, other arithmetic: 50.8 us -> none  [weno_value(): (weight_low * guess_low + weight_mid * guess_mid + weight_high * guess_hi...]
    mul x14 -> x0, local copies, waits for them, and re-layouts: 33.3 us -> none  [the longest x1 23 us: collide(): gain_total = jnp.sum(images[:terms] * images[terms:2 * terms], axis=0)]
    unnamed x57 -> x23, local copies, waits for them, and re-layouts: 37.3 us -> 6.79 us
    slice x15 -> x0, local copies, waits for them, and re-layouts: 24 us -> none  [the longest x2 17.2 us: collide(): loss_part = images[2 * terms]]
where the time goes in v1:
time: 171 us; the launch traced here: 170 us
  Pallas kernels  76.4 us (45%)
  waiting for transfers between devices  57.3 us (34%)
  starting transfers between devices  20 us (12%)
  local copies, waits for them, and re-layouts  13.3 us (8%)
  other arithmetic  1.86 us (1%)
    pallas_call x1, Pallas kernels, collide(): pl.pallas_call(collide_kernel, grid=((count + spare) // GROUP,), in_specs...  34.3 us
    pallas_call x2, Pallas kernels, stage(): pl.pallas_call(functools.partial(stage_kernel, final), grid=(pl.cdiv(widt...  25.8 us
    ppermute x2, waiting for transfers between devices, exchange(): lax.ppermute(strips, 'space', up)  23.4 us
    all_to_all x1, waiting for transfers between devices, shards(): lax.all_to_all(change, 'vel', split_axis=0, concat_axis=0, tiled=True)  13.5 us
    all_to_all x1, waiting for transfers between devices, shards(): got = lax.all_to_all(sent, 'vel', split_axis=0, concat_axis=0, tiled=True)  11.8 us
    ppermute x2, waiting for transfers between devices, exchange(): lax.ppermute(strips, 'space', [(j, i) for i, j in up])  8.58 us
    pallas_call x1, Pallas kernels, pack(): pl.pallas_call(pack_kernel, grid=(pl.cdiv(width, LANES),), in_specs=[lane...  8.32 us
    unnamed x23, local copies, waits for them, and re-layouts  6.79 us
  transfers between devices with their start and end apart: 6, of which 6 were waited for; matrix products, arithmetic and copies ran while one was open for 3% of the time, Pallas kernels for 0%

profile of v1, /device:TPU:1, one launch (start us, length us, event | category | flops | bytes accessed | tf_op | source)
XLA Modules:
  0.0 169.7 jit_solution(2778210305904780587)
XLA Ops:
  0.0 2.7 %copy.12 = f32[1,256,1728]{2,1,0:T(8,128)} copy(f32[1,256,1728]{1,2,0:T(8,128)} %param.9) | data formatting | bytes 3538944 | tf_op args[0]
  2.7 8.3 %shard_map.91 = f32[192,1728]{1,0:T(8,128)} custom-call(f32[256,1728]{1,0:T(8,128)} %bitcast.9), custom_call_target="tpu_custom_call" | custom-call | tf_op jit(solution)/shard_map/pallas_call | solution.py:146
  11.0 4.5 %collective-permute-start = (f32[192,1728]{1,0:T(8,128)}, f32[192,1728]{1,0:T(8,128)S(1)}, u32[]{:S(2)}, u32[]{:S(2)}) collective-permute-start(f32[192,1728]{1,0:T(8,128)} %shard_map.91), channel_id=1, source_target_pairs={{0,8},{8,16},{16,24},{1,9},{9,17},{17,25},{2,10},{10,18},{18,26},{... | collective-permute-start | bytes 3981320 | tf_op jit(solution)/shard_map/ppermute | solution.py:173
  15.6 1.9 %collective-permute-start.1 = (f32[192,1728]{1,0:T(8,128)}, f32[192,1728]{1,0:T(8,128)S(1)}, u32[]{:S(2)}, u32[]{:S(2)}) collective-permute-start(f32[192,1728]{1,0:T(8,128)} %shard_map.91), channel_id=1, source_target_pairs={{8,0},{16,8},{24,16},{9,1},{17,9},{25,17},{10,2},{18,10},{26,18},{... | collective-permute-start | bytes 3981320 | tf_op jit(solution)/shard_map/ppermute | solution.py:173
  17.6 0.7 reshape.159.source_ref
  19.1 0.1 fusion.5
  19.3 0.7 stack.5.refs_3_.refs_4_
  19.9 11.2 %collective-permute-done.refs_1_ = f32[192,1728]{1,0:T(8,128)S(1)} collective-permute-done((f32[192,1728]{1,0:T(8,128)}, f32[192,1728]{1,0:T(8,128)S(1)}, u32[]{:S(2)}, u32[]{:S(2)}) %collective-permute-start) | collective-permute-done | bytes 1327136 | tf_op jit(solution)/shard_map/ppermute | solution.py:173
  31.1 4.3 %collective-permute-done.1.refs_2_ = f32[192,1728]{1,0:T(8,128)S(1)} collective-permute-done((f32[192,1728]{1,0:T(8,128)}, f32[192,1728]{1,0:T(8,128)S(1)}, u32[]{:S(2)}, u32[]{:S(2)}) %collective-permute-start.1) | collective-permute-done | bytes 1327136 | tf_op jit(solution)/shard_map/ppermute | solution.py:173
  35.4 1.1 copy-done.5
  36.5 12.9 %shard_map.92 = (f32[256,1728]{1,0:T(8,128)}, f32[192,1728]{1,0:T(8,128)}) custom-call(f32[12]{0:T(128)} %reshape.159.source_ref, f32[1]{0:T(128)S(6)} %mul.6.ratio_ref, f32[256,1728]{1,0:T(8,128)} %bitcast.10, f32[192,1728]{1,0:T(8,128)} %copy-done.4, f32[192,1728]{1,0:T(8,128)} %copy-done.5, f32[8,1728]{1,0:T(8,128)} %stack.5.refs_3_.refs_4_), custom_call_target="tpu_custom_call" | custom-call | tf_op jit(solution)/shard_map/pallas_call | solution.py:160
  49.4 1.9 %collective-permute-start.2 = (f32[192,1728]{1,0:T(8,128)}, f32[192,1728]{1,0:T(8,128)S(1)}, u32[]{:S(2)}, u32[]{:S(2)}) collective-permute-start(f32[192,1728]{1,0:T(8,128)} %get-tuple-element.8), channel_id=1, source_target_pairs={{0,8},{8,16},{16,24},{1,9},{9,17},{17,25},{2,10},{10,18},{18,26},{... | collective-permute-start | bytes 3981320 | tf_op jit(solution)/shard_map/ppermute | solution.py:173
  51.3 2.5 %collective-permute-start.3 = (f32[192,1728]{1,0:T(8,128)}, f32[192,1728]{1,0:T(8,128)S(1)}, u32[]{:S(2)}, u32[]{:S(2)}) collective-permute-start(f32[192,1728]{1,0:T(8,128)} %get-tuple-element.8), channel_id=1, source_target_pairs={{8,0},{16,8},{24,16},{9,1},{17,9},{25,17},{10,2},{18,10},{26,18},{... | collective-permute-start | bytes 3981320 | tf_op jit(solution)/shard_map/ppermute | solution.py:173
  53.9 0.7 select_reduce_fusion.1.chosen_ref
  54.6 12.2 %collective-permute-done.2.refs_2_ = f32[192,1728]{1,0:T(8,128)S(1)} collective-permute-done((f32[192,1728]{1,0:T(8,128)}, f32[192,1728]{1,0:T(8,128)S(1)}, u32[]{:S(2)}, u32[]{:S(2)}) %collective-permute-start.2) | collective-permute-done | bytes 1327136 | tf_op jit(solution)/shard_map/ppermute | solution.py:173
  66.8 4.3 %collective-permute-done.3.refs_3_ = f32[192,1728]{1,0:T(8,128)S(1)} collective-permute-done((f32[192,1728]{1,0:T(8,128)}, f32[192,1728]{1,0:T(8,128)S(1)}, u32[]{:S(2)}, u32[]{:S(2)}) %collective-permute-start.3) | collective-permute-done | bytes 1327136 | tf_op jit(solution)/shard_map/ppermute | solution.py:173
  71.1 1.1 copy-done.3
  72.2 12.9 %shard_map.93.cells_ref = f32[256,1728]{1,0:T(8,128)} custom-call(f32[12]{0:T(128)} %reshape.159.source_ref, f32[1]{0:T(128)S(6)} %mul.6.ratio_ref, f32[256,1728]{1,0:T(8,128)} %bitcast.11, f32[256,1728]{1,0:T(8,128)} %get-tuple-element.7.refs_1_, f32[192,1728]{1,0:T(8,128)} %copy-done.2, f32[192,1728]{1,0:T(8,128)} %copy-done.3, f32[8,1728]{1,0:T(8,128)} %stack.5.refs_3_.refs_4_), custom_call_target="tpu_custom_call" | custom-call | tf_op jit(solution)/shard_map/pallas_call | solution.py:160
  85.1 3.2 %shard_map.94 = f32[8,3,16,576]{3,2,1,0:T(8,128)} custom-call(s32[128]{0:T(128)} %select_reduce_fusion.1.chosen_ref, f32[256,1728]{1,0:T(8,128)} %shard_map.93.cells_ref), custom_call_target="tpu_custom_call" | custom-call | tf_op jit(solution)/shard_map/pallas_call | solution.py:190
  88.4 5.7 %all-to-all-start = ((f32[8,3,16,576]{3,2,1,0:T(8,128)}), f32[8,3,16,576]{3,2,1,0:T(8,128)S(1)}, u32[]{:S(2)}, u32[]{:S(2)}) async-start(f32[8,3,16,576]{3,2,1,0:T(8,128)} %shard_map.94), calls=%async_computation | async-start | bytes 1966080 | tf_op jit(solution)/shard_map/all_to_all | solution.py:334
  94.0 0.9 reshape.154.first_ref
  94.9 0.9 reshape.155.second_ref
  95.8 0.7 reshape.156.loss_ref
  96.5 11.8 %all-to-all-done = f32[8,3,16,576]{3,2,1,0:T(8,128)S(1)} async-done(((f32[8,3,16,576]{3,2,1,0:T(8,128)}), f32[8,3,16,576]{3,2,1,0:T(8,128)S(1)}, u32[]{:S(2)}, u32[]{:S(2)}) %all-to-all-start) | async-done | bytes 884768 | tf_op jit(solution)/shard_map/all_to_all | solution.py:334
  108.4 0.9 copy-done
  109.3 34.3 %shard_map.95 = f32[24,16,576]{2,1,0:T(8,128)} custom-call(f32[24,16,576]{2,1,0:T(8,128)} %bitcast.13, f32[6,24,576]{2,1,0:T(8,128)} %reshape.154.first_ref, f32[6,24,576]{2,1,0:T(8,128)} %reshape.155.second_ref, f32[24,576]{1,0:T(8,128)} %reshape.156.loss_ref, bf16[2,576,576]{2,1,0:T(8,128)(2,1)} %constant.62.clone.plane_ref, ...), custom_call_target="tpu_custom_call" | custom-call | tf_op jit(solution)/shard_map/pallas_call | solution.py:294
  143.6 3.6 %all-to-all-start.1 = ((f32[8,3,16,576]{3,2,1,0:T(8,128)}), f32[8,3,16,576]{3,2,1,0:T(8,128)S(1)}, u32[]{:S(2)}, u32[]{:S(2)}) async-start(f32[8,3,16,576]{3,2,1,0:T(8,128)} %bitcast.14), calls=%async_computation.1 | async-start | bytes 1966080 | tf_op jit(solution)/shard_map/all_to_all | solution.py:342
  147.2 0.7 reduce_sum.29
  147.9 13.5 %all-to-all-done.1.change_ref = f32[8,3,16,576]{3,2,1,0:T(8,128)S(1)} async-done(((f32[8,3,16,576]{3,2,1,0:T(8,128)}), f32[8,3,16,576]{3,2,1,0:T(8,128)S(1)}, u32[]{:S(2)}, u32[]{:S(2)}) %all-to-all-start.1) | async-done | bytes 884768 | tf_op jit(solution)/shard_map/all_to_all | solution.py:342
  161.4 0.9 copy-done.1
  162.3 4.7 %shard_map.96 = f32[256,1728]{1,0:T(8,128)} custom-call(s32[128]{0:T(128)} %select_reduce_fusion.1.chosen_ref, s32[1]{0:T(128)} %bitcast.count_ref, f32[256,1728]{1,0:T(8,128)} %shard_map.93.cells_ref, f32[8,3,16,576]{3,2,1,0:T(8,128)} %copy-done.1), custom_call_target="tpu_custom_call" | custom-call | tf_op jit(solution)/shard_map/pallas_call | solution.py:217
  167.0 2.7 %copy.13 = f32[1,256,1728]{1,2,0:T(8,128)} copy(f32[1,256,1728]{2,1,0:T(8,128)} %bitcast.12) | data formatting | bytes 3538944 | tf_op jit(solution)/shard_map/reshape | solution.py:343
  (25 shorter events, 0.4 us)
Async XLA Ops:
  2.7 14.8 %copy-start.10 = (s32[1,4]{1,0:T(1,128)S(1)}, s32[1,4]{1,0:T(1,128)}, u32[]{:S(2)}) copy-start(s32[1,4]{1,0:T(1,128)} %param.10) | copy-start | bytes 52
  11.0 20.1 %collective-permute-start = (f32[192,1728]{1,0:T(8,128)}, f32[192,1728]{1,0:T(8,128)S(1)}, u32[]{:S(2)}, u32[]{:S(2)}) collective-permute-start(f32[192,1728]{1,0:T(8,128)} %shard_map.91), channel_id=1, source_target_pairs={{0,8},{8,16},{16,24},{1,9},{9,17},{17,25},{2,10},{10,18},{18,26},{... | collective-permute-start | bytes 3981320 | tf_op jit(solution)/shard_map/ppermute | solution.py:173
  15.6 19.8 %collective-permute-start.1 = (f32[192,1728]{1,0:T(8,128)}, f32[192,1728]{1,0:T(8,128)S(1)}, u32[]{:S(2)}, u32[]{:S(2)}) collective-permute-start(f32[192,1728]{1,0:T(8,128)} %shard_map.91), channel_id=1, source_target_pairs={{8,0},{16,8},{24,16},{9,1},{17,9},{25,17},{10,2},{18,10},{26,18},{... | collective-permute-start | bytes 3981320 | tf_op jit(solution)/shard_map/ppermute | solution.py:173
  19.9 33.8 %copy-start.9 = (s32[256]{0:T(256)S(1)}, s32[256]{0:T(256)}, u32[]{:S(2)}) copy-start(s32[256]{0:T(256)} %param.12) | copy-start | bytes 3076
  31.1 4.3 %copy-start.4 = (f32[192,1728]{1,0:T(8,128)}, f32[192,1728]{1,0:T(8,128)S(1)}, u32[]{:S(2)}) copy-start(f32[192,1728]{1,0:T(8,128)S(1)} %collective-permute-done.refs_1_) | copy-start | bytes 3981316
  35.4 1.1 copy-start.5
  49.4 17.5 %collective-permute-start.2 = (f32[192,1728]{1,0:T(8,128)}, f32[192,1728]{1,0:T(8,128)S(1)}, u32[]{:S(2)}, u32[]{:S(2)}) collective-permute-start(f32[192,1728]{1,0:T(8,128)} %get-tuple-element.8), channel_id=1, source_target_pairs={{0,8},{8,16},{16,24},{1,9},{9,17},{17,25},{2,10},{10,18},{18,26},{... | collective-permute-start | bytes 3981320 | tf_op jit(solution)/shard_map/ppermute | solution.py:173
  51.3 19.8 %collective-permute-start.3 = (f32[192,1728]{1,0:T(8,128)}, f32[192,1728]{1,0:T(8,128)S(1)}, u32[]{:S(2)}, u32[]{:S(2)}) collective-permute-start(f32[192,1728]{1,0:T(8,128)} %get-tuple-element.8), channel_id=1, source_target_pairs={{8,0},{16,8},{24,16},{9,1},{17,9},{25,17},{10,2},{18,10},{26,18},{... | collective-permute-start | bytes 3981320 | tf_op jit(solution)/shard_map/ppermute | solution.py:173
  66.8 4.3 %copy-start.2 = (f32[192,1728]{1,0:T(8,128)}, f32[192,1728]{1,0:T(8,128)S(1)}, u32[]{:S(2)}) copy-start(f32[192,1728]{1,0:T(8,128)S(1)} %collective-permute-done.2.refs_2_) | copy-start | bytes 3981316
  71.1 1.1 copy-start.3
  88.4 5.7 %copy-start.6 = (f32[6,13824]{1,0:T(8,128)S(1)}, f32[6,13824]{1,0:T(8,128)}, u32[]{:S(2)}) copy-start(f32[6,13824]{1,0:T(8,128)} %param.13) | copy-start | bytes 995332
  88.4 6.6 %copy-start.7 = (f32[6,13824]{1,0:T(8,128)S(1)}, f32[6,13824]{1,0:T(8,128)}, u32[]{:S(2)}) copy-start(f32[6,13824]{1,0:T(8,128)} %param.14) | copy-start | bytes 995332
  88.4 7.4 %copy-start.8 = (f32[13824]{0:T(1024)S(1)}, f32[13824]{0:T(1024)}, u32[]{:S(2)}) copy-start(f32[13824]{0:T(1024)} %param.15) | copy-start | bytes 165892
  88.4 20.0 %all-to-all-start = ((f32[8,3,16,576]{3,2,1,0:T(8,128)}), f32[8,3,16,576]{3,2,1,0:T(8,128)S(1)}, u32[]{:S(2)}, u32[]{:S(2)}) async-start(f32[8,3,16,576]{3,2,1,0:T(8,128)} %shard_map.94), calls=%async_computation | async-start | bytes 1966080 | tf_op jit(solution)/shard_map/all_to_all | solution.py:334
  108.4 0.9 copy-start
  143.6 17.8 %all-to-all-start.1 = ((f32[8,3,16,576]{3,2,1,0:T(8,128)}), f32[8,3,16,576]{3,2,1,0:T(8,128)S(1)}, u32[]{:S(2)}, u32[]{:S(2)}) async-start(f32[8,3,16,576]{3,2,1,0:T(8,128)} %bitcast.14), calls=%async_computation.1 | async-start | bytes 1966080 | tf_op jit(solution)/shard_map/all_to_all | solution.py:342
  161.4 0.9 copy-start.1

commit v2 on v1

--- a/solution.py
+++ b/solution.py
@@ -28,15 +28,21 @@
     return jnp.stack(rows + [jnp.zeros_like(first)] * 4)
 
 
-def pack_kernel(u_ref, pack_ref):
+def pack_strips(cells_ref, against_first, against_second, strips_ref):
     side = BSIDE
-    pack_ref[0 : 3 * side] = u_ref[0 : 3 * side]
-    pack_ref[3 * side : 6 * side] = u_ref[(side - 3) * side :]
-    for layer in range(3):
-        at = (6 + layer) * side
-        pack_ref[at : at + side] = u_ref[pl.ds(layer, side, stride=side), :]
-        at = (9 + layer) * side
-        pack_ref[at : at + side] = u_ref[pl.ds(side - 3 + layer, side, stride=side), :]
+
+    def first(n):
+        return cells_ref[n * side : (n + 1) * side]
+
+    def second(n):
+        return cells_ref[pl.ds(n, side, stride=side), :]
+
+    at = 0
+    for line, against in ((first, against_first), (second, against_second)):
+        far = jnp.where(against, line(2), line(side - 3))
+        for layer in (line(0), line(1), far, line(side - 2), line(side - 1)):
+            strips_ref[at : at + side] = layer
+            at += side
 
 
 def sweep(line, against, speed, flux_ref):
@@ -82,13 +88,10 @@
         before = edge
 
 
-def stage_kernel(final, source_ref, ratio_ref, *refs):
-    if final:
-        base_ref, u_ref, left_ref, right_ref, speed_ref, out_ref, flux_one, flux_two, flux_turned = refs
-    else:
-        u_ref, left_ref, right_ref, speed_ref, out_ref, pack_ref, flux_one, flux_two, flux_turned = refs
+def advance(source_ref, ratio, u_ref, base_ref, left_ref, right_ref, speed_ref, out_ref, fluxes):
     side = BSIDE
     lanes = u_ref.shape[1]
+    flux_one, flux_two, flux_turned = fluxes
 
     def first_line(n):
         return u_ref[n * side : (n + 1) * side]
@@ -96,91 +99,203 @@
     def second_line(n):
         return u_ref[pl.ds(n, side, stride=side), :]
 
-    def ghost(face, strip, layer, own):
-        at = (3 * strip + layer) * side
+    def ghost(face, block, own):
+        at = block * side
         return (
             source_ref[3 * face] * left_ref[at : at + side]
             + source_ref[3 * face + 1] * own
             + source_ref[3 * face + 2] * right_ref[at : at + side]
         )
 
-    def padded(line, faces, strips):
+    def padded(line, faces, start):
         ghosts = {}
         for layer in range(3):
-            ghosts[layer] = ghost(faces[0], strips[0], layer, line(side - 3 + layer))
-            ghosts[side + 3 + layer] = ghost(faces[1], strips[1], layer, line(layer))
+            ghosts[layer] = ghost(faces[0], start + 2 + layer, line(side - 3 + layer))
+            ghosts[side + 3 + layer] = ghost(faces[1], start + layer, line(layer))
         return lambda n: ghosts[n] if n in ghosts else line(n - 3)
 
-    def spread(row):
-        return jnp.broadcast_to(speed_ref[row : row + 1], (side, lanes))
-
-    against_first = spread(2) > 0.5
-    against_second = spread(3) > 0.5
-    sweep(padded(first_line, (0, 1), (1, 0)), against_first, spread(0), flux_one)
-    sweep(padded(second_line, (2, 3), (3, 2)), against_second, spread(1), flux_two)
+    against_first, against_second = against_masks(speed_ref)
+    sweep(padded(first_line, (0, 1), 0), against_first, spread(speed_ref, 0), flux_one)
+    sweep(padded(second_line, (2, 3), 5), against_second, spread(speed_ref, 1), flux_two)
     for n in range(side):
         back = side - 1 - n
         flux_turned[n * side : (n + 1) * side] = jnp.where(
             against_second, flux_two[back * side : (back + 1) * side], flux_two[n * side : (n + 1) * side]
         )
-    ratio = ratio_ref[0]
     for n in range(side):
         back = side - 1 - n
         rows = slice(n * side, (n + 1) * side)
         change = jnp.where(against_first, flux_one[back * side : (back + 1) * side], flux_one[rows])
         change = change + flux_turned[pl.ds(n, side, stride=side), :]
         moved = u_ref[rows] - ratio * change
-        if final:
+        if base_ref is not None:
             moved = 0.5 * base_ref[rows] + 0.5 * moved
         out_ref[rows] = moved
-    if not final:
-        pack_kernel(out_ref, pack_ref)
-
-
-def lane_spec(rows):
-    return pl.BlockSpec((rows, LANES), lambda n: (0, n))
-
-
-def pack(cells):
-    count, width = cells.shape
+
+
+def spread(speed_ref, row):
+    return jnp.broadcast_to(speed_ref[row : row + 1], (BSIDE, speed_ref.shape[1]))
+
+
+def against_masks(speed_ref):
+    return spread(speed_ref, 2) > 0.5, spread(speed_ref, 3) > 0.5
+
+
+def transport_kernel(
+    source_ref, ratio_ref, u_ref, speed_ref, out_ref,
+    one_ref, flux_one, flux_two, flux_turned,
+    strips, from_left, from_right, sent_left, sent_right, got_left, got_right,
+):
+    tiles = u_ref.shape[0]
+    me = lax.axis_index("space")
+    count = lax.axis_size("space")
+    has_left, has_right = me > 0, me < count - 1
+    left, right = lax.rem(me + count - 1, count), lax.rem(me + 1, count)
+    mesh_ids = pl.DeviceIdType.MESH
+    ratio = ratio_ref[0]
+    fluxes = (flux_one, flux_two, flux_turned)
+
+    barrier = pltpu.get_barrier_semaphore()
+
+    @pl.when(has_left)
+    def _():
+        pl.semaphore_signal(barrier, inc=1, device_id={"space": left}, device_id_type=mesh_ids)
+
+    @pl.when(has_right)
+    def _():
+        pl.semaphore_signal(barrier, inc=1, device_id={"space": right}, device_id_type=mesh_ids)
+
+    pl.semaphore_wait(barrier, has_left.astype(jnp.int32) + has_right.astype(jnp.int32))
+
+    def to_right(turn, tile):
+        return pltpu.make_async_remote_copy(
+            src_ref=strips.at[turn, tile], dst_ref=from_left.at[turn, tile],
+            send_sem=sent_right.at[turn, tile], recv_sem=got_left.at[turn, tile],
+            device_id={"space": right}, device_id_type=mesh_ids,
+        )
+
+    def to_left(turn, tile):
+        return pltpu.make_async_remote_copy(
+            src_ref=strips.at[turn, tile], dst_ref=from_right.at[turn, tile],
+            send_sem=sent_left.at[turn, tile], recv_sem=got_right.at[turn, tile],
+            device_id={"space": left}, device_id_type=mesh_ids,
+        )
+
+    def send(turn, tile, cells_ref):
+        pack_strips(cells_ref.at[tile], *against_masks(speed_ref.at[tile]), strips.at[turn, tile])
+
+        @pl.when(has_right)
+        def _():
+            to_right(turn, tile).start()
+
+        @pl.when(has_left)
+        def _():
+            to_left(turn, tile).start()
+
+    def receive(turn, tile):
+        @pl.when(has_left)
+        def _():
+            to_right(turn, tile).wait_recv()
+
+        @pl.when(has_right)
+        def _():
+            to_left(turn, tile).wait_recv()
+
+    def begin(tile, carry):
+        send(0, tile, u_ref)
+        return carry
+
+    lax.fori_loop(0, tiles, begin, 0)
+
+    @pl.when(me == 0)
+    def _():
+        from_left[...] = jnp.zeros_like(from_left)
+
+    @pl.when(me == count - 1)
+    def _():
+        from_right[...] = jnp.zeros_like(from_right)
+
+    def first(tile, carry):
+        receive(0, tile)
+        advance(
+            source_ref, ratio, u_ref.at[tile], None, from_left.at[0, tile], from_right.at[0, tile],
+            speed_ref.at[tile], one_ref.at[tile], fluxes,
+        )
+        send(1, tile, one_ref)
+        return carry
+
+    lax.fori_loop(0, tiles, first, 0)
+
+    def second(tile, carry):
+        receive(1, tile)
+        advance(
+            source_ref, ratio, one_ref.at[tile], u_ref.at[tile], from_left.at[1, tile], from_right.at[1, tile],
+            speed_ref.at[tile], out_ref.at[tile], fluxes,
+        )
+        return carry
+
+    lax.fori_loop(0, tiles, second, 0)
+
+    def finish(tile, carry):
+        for turn in range(2):
+
+            @pl.when(has_right)
+            def _():
+                to_right(turn, tile).wait_send()
+
+            @pl.when(has_left)
+            def _():
+                to_left(turn, tile).wait_send()
+
+        return carry
+
+    lax.fori_loop(0, tiles, finish, 0)
+
+
+def transport(source, ratio, cells, speeds):
+    tiles, count, lanes = cells.shape
+    smem = pl.BlockSpec(memory_space=pltpu.SMEM)
+    vmem = pl.BlockSpec(memory_space=pltpu.VMEM)
+    strips = pltpu.VMEM((2, tiles, 10 * BSIDE, lanes), jnp.float32)
     return pl.pallas_call(
-        pack_kernel,
-        grid=(pl.cdiv(width, LANES),),
-        in_specs=[lane_spec(count)],
-        out_specs=lane_spec(12 * BSIDE),
-        out_shape=jax.ShapeDtypeStruct((12 * BSIDE, width), jnp.float32),
-    )(cells)
-
-
-def stage(final, source, ratio, arrays):
-    count, width = arrays[0].shape
-    smem = pl.BlockSpec(memory_space=pltpu.SMEM)
-    full = jax.ShapeDtypeStruct((count, width), jnp.float32)
-    strips = jax.ShapeDtypeStruct((12 * BSIDE, width), jnp.float32)
-    return pl.pallas_call(
-        functools.partial(stage_kernel, final),
-        grid=(pl.cdiv(width, LANES),),
-        in_specs=[smem, smem] + [lane_spec(array.shape[0]) for array in arrays],
-        out_specs=lane_spec(count) if final else [lane_spec(count), lane_spec(12 * BSIDE)],
-        out_shape=full if final else [full, strips],
-        scratch_shapes=[pltpu.VMEM((count, LANES), jnp.float32)] * 3,
-    )(source, ratio, *arrays)
-
-
-def exchange(strips):
-    count = lax.axis_size("space")
-    up = [(i, i + 1) for i in range(count - 1)]
-    return lax.ppermute(strips, "space", up), lax.ppermute(strips, "space", [(j, i) for i, j in up])
-
-
-def gather_kernel(chosen_ref, cells_ref, out_ref, rows_ref):
+        transport_kernel,
+        in_specs=[smem, smem, vmem, vmem],
+        out_specs=vmem,
+        out_shape=jax.ShapeDtypeStruct(cells.shape, jnp.float32),
+        scratch_shapes=[pltpu.VMEM(cells.shape, jnp.float32)]
+        + [pltpu.VMEM((count, lanes), jnp.float32)] * 3
+        + [strips] * 3
+        + [pltpu.SemaphoreType.DMA((2, tiles))] * 4,
+        compiler_params=pltpu.CompilerParams(
+            collective_id=0, has_side_effects=True, vmem_limit_bytes=48 * 1024 * 1024
+        ),
+    )(source, ratio, cells, speeds)
+
+
+def tiled(rows):
+    count, width = rows.shape
+    tiles = pl.cdiv(width, LANES)
+    rows = jnp.pad(rows, ((0, 0), (0, tiles * LANES - width)))
+    return rows.reshape(count, tiles, LANES).transpose(1, 0, 2)
+
+
+def lane_pieces(tiles, width):
+    return [(t, t * LANES, min(width, (t + 1) * LANES)) for t in range(tiles)]
+
+
+def gather_kernel(chosen_ref, cells_ref, out_ref, picked_ref, rows_ref):
     parts, planes, each, plane = out_ref.shape
+    tiles = cells_ref.shape[0]
 
     def one(slot, carry):
-        rows_ref[pl.ds(slot, 1), :] = cells_ref[pl.ds(chosen_ref[slot], 1), :]
+        row = chosen_ref[slot]
+        for tile in range(tiles):
+            picked_ref[tile, pl.ds(slot, 1), :] = cells_ref[tile, pl.ds(row, 1), :]
         return carry
 
     lax.fori_loop(0, parts * each, one, 0, unroll=8)
+    for tile in range(tiles):
+        rows_ref[:, tile * LANES : (tile + 1) * LANES] = picked_ref[tile]
     for part in range(parts):
         for n in range(planes):
             out_ref[part, n] = rows_ref[part * each : (part + 1) * each, n * plane : (n + 1) * plane]
@@ -192,20 +307,24 @@
         in_specs=[pl.BlockSpec(memory_space=pltpu.SMEM), pl.BlockSpec(memory_space=pltpu.VMEM)],
         out_specs=pl.BlockSpec(memory_space=pltpu.VMEM),
         out_shape=jax.ShapeDtypeStruct(shape, jnp.float32),
-        scratch_shapes=[pltpu.VMEM((shape[0] * shape[2], cells.shape[1]), jnp.float32)],
+        scratch_shapes=[
+            pltpu.VMEM((cells.shape[0], shape[0] * shape[2], LANES), jnp.float32),
+            pltpu.VMEM((shape[0] * shape[2], cells.shape[0] * LANES), jnp.float32),
+        ],
     )(chosen, cells)
 
 
 def scatter_kernel(chosen_ref, count_ref, cells_ref, change_ref, out_ref, rows_ref):
     parts, planes, each, plane = change_ref.shape
+    for tile, begin, end in lane_pieces(cells_ref.shape[0], out_ref.shape[1]):
+        out_ref[:, begin:end] = cells_ref[tile, :, : end - begin]
     for part in range(parts):
         for n in range(planes):
             rows_ref[part * each : (part + 1) * each, n * plane : (n + 1) * plane] = change_ref[part, n]
-    out_ref[...] = cells_ref[...]
 
     def one(slot, carry):
         row = pl.ds(chosen_ref[slot], 1)
-        out_ref[row, :] = cells_ref[row, :] + rows_ref[pl.ds(slot, 1), :]
+        out_ref[row, :] += rows_ref[pl.ds(slot, 1), :]
         return carry
 
     lax.fori_loop(0, count_ref[0], one, 0)
@@ -214,12 +333,13 @@
 def scatter(chosen, count, cells, change):
     smem = pl.BlockSpec(memory_space=pltpu.SMEM)
     vmem = pl.BlockSpec(memory_space=pltpu.VMEM)
+    parts, planes, each, plane = change.shape
     return pl.pallas_call(
         scatter_kernel,
         in_specs=[smem, smem, vmem, vmem],
         out_specs=vmem,
-        out_shape=jax.ShapeDtypeStruct(cells.shape, jnp.float32),
-        scratch_shapes=[pltpu.VMEM((change.shape[0] * change.shape[2], cells.shape[1]), jnp.float32)],
+        out_shape=jax.ShapeDtypeStruct((cells.shape[1], planes * plane), jnp.float32),
+        scratch_shapes=[pltpu.VMEM((parts * each, planes * plane), jnp.float32)],
     )(chosen, count, cells, change)
 
 
@@ -229,32 +349,38 @@
     return high, low
 
 
-def dot3(left, right):
-    def dot(a, b):
-        return jnp.dot(a, b, preferred_element_type=jnp.float32)
-
-    return dot(left[0], right[0]) + (dot(left[1], right[0]) + dot(left[0], right[1]))
+def dot(left, right):
+    return jnp.dot(left, right, preferred_element_type=jnp.float32)
 
 
 def collide_kernel(cells_ref, first_ref, second_ref, loss_ref, plane_ref, line_ref, out_ref):
     depth, group, plane = cells_ref.shape
     terms = first_ref.shape[0]
-    plane_table = (plane_ref[0], plane_ref[1])
-    line_table = (line_ref[0], line_ref[1])
-
-    def transform(flat):
-        return dot3(line_table, halves(dot3(halves(flat), plane_table)))
-
-    values = cells_ref[...].reshape(depth * group, plane)
-    spectrum = transform(values).reshape(depth, group, plane)
-
-    def image(multiplier):
-        return transform((spectrum * multiplier[:, None, :]).reshape(depth * group, plane))
-
-    total = -values * image(loss_ref[...])
+    size = depth * group
+
+    def transforms(cubes):
+        high, low = halves(jnp.concatenate(cubes, axis=0) if len(cubes) > 1 else cubes[0])
+        rows = high.shape[0]
+        wide = dot(jnp.concatenate([high, low], axis=0), plane_ref[0])
+        mapped = wide[:rows] + (wide[rows:] + dot(high, plane_ref[1]))
+        results = []
+        for n in range(len(cubes)):
+            high, low = halves(mapped[n * size : (n + 1) * size])
+            wide = dot(line_ref[...], high)
+            results.append(wide[:size] + (wide[size:] + dot(line_ref[:size], low)))
+        return results
+
+    values = cells_ref[...].reshape(size, plane)
+    spectrum = transforms([values])[0].reshape(depth, group, plane)
+
+    def scaled(multiplier):
+        return (spectrum * multiplier[:, None, :]).reshape(size, plane)
+
+    total = -values * transforms([scaled(loss_ref[...])])[0]
 
     def one(term, total):
-        return total + image(first_ref[term]) * image(second_ref[term])
+        image_one, image_two = transforms([scaled(first_ref[term]), scaled(second_ref[term])])
+        return total + image_one * image_two
 
     total = lax.fori_loop(0, terms, one, total)
     out_ref[...] = total.reshape(depth, group, plane)
@@ -270,7 +396,7 @@
         high = wide.astype(jnp.bfloat16)
         return np.stack([high, (wide - high.astype(np.float32)).astype(jnp.bfloat16)])
 
-    return split(np.kron(table, table)), split(np.kron(table, np.eye(GROUP)))
+    return split(np.kron(table, table)), np.concatenate(split(np.kron(table, np.eye(GROUP))))
 
 
 def collide(cells, gain_first, gain_second, loss_rates):
@@ -314,8 +440,7 @@
     source = (offset[:, None] == jnp.arange(3)) & (neighbours[0] >= 0)[:, None]
     source = source.astype(jnp.float32).reshape(-1)
 
-    section_one, strips = stage(False, source, ratio, (density, *exchange(pack(density)), speeds))
-    section_two = stage(True, source, ratio, (density, section_one, *exchange(strips), speeds))
+    section_two = transport(source, ratio, tiled(density), tiled(speeds))
 
     parts = lax.axis_size("vel")
     each = ACT // parts

time: 171 us -> 132 us (0.77)
  waiting for transfers between devices: 57.3 us -> 33 us
  starting transfers between devices: 20 us -> 9.34 us
  Pallas kernels: 76.4 us -> 71.2 us
  other arithmetic: 1.86 us -> 4.47 us
    ppermute x4 -> x0, waiting for transfers between devices: 32 us -> none  [the longest x2 23.4 us: exchange(): lax.ppermute(strips, 'space', up)]
    ppermute x4 -> x0, starting transfers between devices: 10.8 us -> none  [the longest x2 6.42 us: exchange(): lax.ppermute(strips, 'space', up)]
    all_to_all x1, waiting for transfers between devices: 13.5 us -> 19.8 us  [shards(): lax.all_to_all(change, 'vel', split_axis=0, concat_axis=0, tiled=True)]
    unnamed x23 -> x14, local copies, waits for them, and re-layouts: 6.79 us -> 3.15 us
    pallas_call x3 -> x1, Pallas kernels: 34.1 us -> 30.7 us  [transport(): pl.pallas_call(transport_kernel, in_specs=[smem, smem, vmem, vmem], out_s...]
    pad x0 -> x1, local copies, waits for them, and re-layouts: none -> 2.85 us  [tiled(): rows = jnp.pad(rows, ((0, 0), (0, tiles * LANES - width)))]
    pallas_call x1, Pallas kernels: 34.3 us -> 31.7 us  [collide(): pl.pallas_call(collide_kernel, grid=((count + spare) // GROUP,), in_specs...]
    reshape x0 -> x1, local copies, waits for them, and re-layouts: none -> 1.79 us  [tiled(): return rows.reshape(count, tiles, LANES).transpose(1, 0, 2)]
  transfers between devices with their start and end apart: 6 -> 2, of which waited for: 6 -> 2; matrix products, arithmetic and copies ran while one was open for 3% -> 2% of each run, Pallas kernels for 0% -> 0%
where the time goes in v2:
time: 132 us
  Pallas kernels  71.2 us (54%)
  waiting for transfers between devices  33 us (25%)
  local copies, waits for them, and re-layouts  13.1 us (10%)
  starting transfers between devices  9.34 us (7%)
  other arithmetic  4.47 us (3%)
    pallas_call x1, Pallas kernels, collide(): pl.pallas_call(collide_kernel, grid=((count + spare) // GROUP,), in_specs...  31.7 us
    pallas_call x1, Pallas kernels, transport(): pl.pallas_call(transport_kernel, in_specs=[smem, smem, vmem, vmem], out_s...  30.7 us
    all_to_all x1, waiting for transfers between devices, shards(): lax.all_to_all(change, 'vel', split_axis=0, concat_axis=0, tiled=True)  19.8 us
    all_to_all x1, waiting for transfers between devices, shards(): got = lax.all_to_all(sent, 'vel', split_axis=0, concat_axis=0, tiled=True)  13.1 us
    all_to_all x1, starting transfers between devices, shards(): got = lax.all_to_all(sent, 'vel', split_axis=0, concat_axis=0, tiled=True)  5.66 us
    pallas_call x1, Pallas kernels, scatter(): pl.pallas_call(scatter_kernel, in_specs=[smem, smem, vmem, vmem], out_spe...  5.11 us
    all_to_all x1, starting transfers between devices, shards(): lax.all_to_all(change, 'vel', split_axis=0, concat_axis=0, tiled=True)  3.69 us
    pallas_call x1, Pallas kernels, gather(): pl.pallas_call(gather_kernel, in_specs=[pl.BlockSpec(memory_space=pltpu.S...  3.68 us
  transfers between devices with their start and end apart: 2, of which 2 were waited for; matrix products, arithmetic and copies ran while one was open for 2% of the time, Pallas kernels for 0%

profile of v2, /device:TPU:1, one launch (start us, length us, event | category | flops | bytes accessed | tf_op | source)
XLA Modules:
  0.0 131.9 jit_solution(15674246955919551483)
XLA Ops:
  0.0 0.7 broadcast_compare_fusion
  0.7 0.8 select_reduce_fusion
  1.5 0.1 fusion.5
  1.6 0.1 compare_select_fusion
  2.4 0.7 compare_bitcast_fusion
  3.1 0.7 subtract_bitcast_fusion
  3.8 0.1 fusion.8
  3.8 0.1 reshape.167.source_ref
  3.9 0.1 stack.5
  4.0 2.9 %pad.8 = f32[256,1792]{0,1:T(8,128)} pad(f32[256,1728]{0,1:T(8,128)} %bitcast.20, f32[]{:T(128)} %constant.54.clone.1), padding=0_0x0_64 | pad | bytes 3604484 | tf_op jit(solution)/shard_map/jit(_pad)/pad | solution.py:278
  6.9 1.8 %copy.13 = f32[256,14,128]{2,0,1:T(8,128)S(1)} copy(f32[256,14,128]{0,2,1:T(8,128)} %bitcast.17) | data formatting | bytes 3670016 | tf_op jit(solution)/shard_map/reshape | solution.py:279
  8.7 0.7 select_reduce_fusion.1.chosen_ref
  9.4 30.7 %shard_map.91.cells_ref = f32[14,256,128]{2,1,0:T(8,128)S(1)} custom-call(f32[12]{0:T(128)S(1)} %reshape.167.source_ref, f32[1]{0:T(128)S(6)} %mul.6.ratio_ref, f32[14,256,128]{2,1,0:T(8,128)S(1)} %bitcast.15, f32[14,8,128]{2,1,0:T(8,128)S(1)} %pad_bitcast_fusion.speed_ref), custom_call_target="tpu_custom_call" | custom-call | tf_op jit(solution)/shard_map/pallas_call | solution.py:260
  40.1 0.0 copy-start
  40.1 1.2 copy-done
  41.4 3.7 %shard_map.92 = f32[8,3,16,576]{3,2,1,0:T(8,128)} custom-call(s32[128]{0:T(128)} %select_reduce_fusion.1.chosen_ref, f32[14,256,128]{2,1,0:T(8,128)} %copy-done), custom_call_target="tpu_custom_call" | custom-call | tf_op jit(solution)/shard_map/pallas_call | solution.py:305
  45.1 5.7 %all-to-all-start = ((f32[8,3,16,576]{3,2,1,0:T(8,128)}), f32[8,3,16,576]{3,2,1,0:T(8,128)S(1)}, u32[]{:S(2)}, u32[]{:S(2)}) async-start(f32[8,3,16,576]{3,2,1,0:T(8,128)} %shard_map.92), calls=%async_computation | async-start | bytes 1966080 | tf_op jit(solution)/shard_map/all_to_all | solution.py:459
  50.7 0.0 copy-done.5
  50.7 0.7 reshape.164.loss_ref
  51.4 0.0 copy-done.3
  51.4 0.9 reshape.162.first_ref
  52.3 0.0 copy-done.4
  52.3 0.9 reshape.163.second_ref
  53.2 13.1 %all-to-all-done = f32[8,3,16,576]{3,2,1,0:T(8,128)S(1)} async-done(((f32[8,3,16,576]{3,2,1,0:T(8,128)}), f32[8,3,16,576]{3,2,1,0:T(8,128)S(1)}, u32[]{:S(2)}, u32[]{:S(2)}) %all-to-all-start) | async-done | bytes 884768 | tf_op jit(solution)/shard_map/all_to_all | solution.py:459
  66.3 0.9 copy-done.1
  67.2 31.7 %shard_map.93 = f32[24,16,576]{2,1,0:T(8,128)} custom-call(f32[24,16,576]{2,1,0:T(8,128)} %bitcast.18, f32[6,24,576]{2,1,0:T(8,128)} %reshape.162.first_ref, f32[6,24,576]{2,1,0:T(8,128)} %reshape.163.second_ref, f32[24,576]{1,0:T(8,128)} %reshape.164.loss_ref, bf16[2,576,576]{2,1,0:T(8,128)(2,1)} %constant.63.clone.plane_ref, ...), custom_call_target="tpu_custom_call" | custom-call | tf_op jit(solution)/shard_map/pallas_call | solution.py:420
  99.0 3.7 %all-to-all-start.1 = ((f32[8,3,16,576]{3,2,1,0:T(8,128)}), f32[8,3,16,576]{3,2,1,0:T(8,128)S(1)}, u32[]{:S(2)}, u32[]{:S(2)}) async-start(f32[8,3,16,576]{3,2,1,0:T(8,128)} %bitcast.19), calls=%async_computation.1 | async-start | bytes 1966080 | tf_op jit(solution)/shard_map/all_to_all | solution.py:467
  102.7 0.6 reduce_sum.29
  103.3 19.8 %all-to-all-done.1.change_ref = f32[8,3,16,576]{3,2,1,0:T(8,128)S(1)} async-done(((f32[8,3,16,576]{3,2,1,0:T(8,128)}), f32[8,3,16,576]{3,2,1,0:T(8,128)S(1)}, u32[]{:S(2)}, u32[]{:S(2)}) %all-to-all-start.1) | async-done | bytes 884768 | tf_op jit(solution)/shard_map/all_to_all | solution.py:467
  123.1 0.9 copy-done.2
  124.0 5.1 %shard_map.94 = f32[256,1728]{1,0:T(8,128)} custom-call(s32[128]{0:T(128)} %select_reduce_fusion.1.chosen_ref, s32[1]{0:T(128)} %bitcast.count_ref, f32[14,256,128]{2,1,0:T(8,128)} %copy-done, f32[8,3,16,576]{3,2,1,0:T(8,128)} %copy-done.2), custom_call_target="tpu_custom_call" | custom-call | tf_op jit(solution)/shard_map/pallas_call | solution.py:337
  129.2 2.7 %copy.14 = f32[1,256,1728]{1,2,0:T(8,128)} copy(f32[1,256,1728]{2,1,0:T(8,128)} %bitcast.16) | data formatting | bytes 3538944 | tf_op jit(solution)/shard_map/reshape | solution.py:468
  (9 shorter events, 0.0 us)
Async XLA Ops:
  40.1 1.3 copy-start
  41.4 9.3 %copy-start.5 = (f32[13824]{0:T(1024)S(1)}, f32[13824]{0:T(1024)}, u32[]{:S(2)}) copy-start(f32[13824]{0:T(1024)} %param.15) | copy-start | bytes 165892
  41.4 10.1 %copy-start.3 = (f32[6,13824]{1,0:T(8,128)S(1)}, f32[6,13824]{1,0:T(8,128)}, u32[]{:S(2)}) copy-start(f32[6,13824]{1,0:T(8,128)} %param.13) | copy-start | bytes 995332
  45.1 7.3 %copy-start.4 = (f32[6,13824]{1,0:T(8,128)S(1)}, f32[6,13824]{1,0:T(8,128)}, u32[]{:S(2)}) copy-start(f32[6,13824]{1,0:T(8,128)} %param.14) | copy-start | bytes 995332
  45.1 21.2 %all-to-all-start = ((f32[8,3,16,576]{3,2,1,0:T(8,128)}), f32[8,3,16,576]{3,2,1,0:T(8,128)S(1)}, u32[]{:S(2)}, u32[]{:S(2)}) async-start(f32[8,3,16,576]{3,2,1,0:T(8,128)} %shard_map.92), calls=%async_computation | async-start | bytes 1966080 | tf_op jit(solution)/shard_map/all_to_all | solution.py:459
  66.3 0.9 copy-start.1
  99.0 3.7 %copy-start.6 = (s32[256]{0:T(256)S(1)}, s32[256]{0:T(256)}, u32[]{:S(2)}) copy-start(s32[256]{0:T(256)} %param.12) | copy-start | bytes 3076
  99.0 24.1 %all-to-all-start.1 = ((f32[8,3,16,576]{3,2,1,0:T(8,128)}), f32[8,3,16,576]{3,2,1,0:T(8,128)S(1)}, u32[]{:S(2)}, u32[]{:S(2)}) async-start(f32[8,3,16,576]{3,2,1,0:T(8,128)} %bitcast.19), calls=%async_computation.1 | async-start | bytes 1966080 | tf_op jit(solution)/shard_map/all_to_all | solution.py:467
  123.1 0.9 copy-start.2

commit v3 on v2

--- a/solution.py
+++ b/solution.py
@@ -353,10 +353,10 @@
     return jnp.dot(left, right, preferred_element_type=jnp.float32)
 
 
-def collide_kernel(cells_ref, first_ref, second_ref, loss_ref, plane_ref, line_ref, out_ref):
-    depth, group, plane = cells_ref.shape
-    terms = first_ref.shape[0]
-    size = depth * group
+def collision(values, tables, depth):
+    first_ref, second_ref, loss_ref, plane_ref, line_ref = tables
+    size, plane = values.shape
+    group = size // depth
 
     def transforms(cubes):
         high, low = halves(jnp.concatenate(cubes, axis=0) if len(cubes) > 1 else cubes[0])
@@ -370,7 +370,6 @@
             results.append(wide[:size] + (wide[size:] + dot(line_ref[:size], low)))
         return results
 
-    values = cells_ref[...].reshape(size, plane)
     spectrum = transforms([values])[0].reshape(depth, group, plane)
 
     def scaled(multiplier):
@@ -382,8 +381,68 @@
         image_one, image_two = transforms([scaled(first_ref[term]), scaled(second_ref[term])])
         return total + image_one * image_two
 
-    total = lax.fori_loop(0, terms, one, total)
+    return lax.fori_loop(0, first_ref.shape[0], one, total)
+
+
+def collide_kernel(cells_ref, *refs):
+    depth, group, plane = cells_ref.shape
+    out_ref = refs[-1]
+    total = collision(cells_ref[...].reshape(depth * group, plane), refs[:-1], depth)
     out_ref[...] = total.reshape(depth, group, plane)
+
+
+def swap_collide_kernel(
+    cells_ref, first_ref, second_ref, loss_ref, plane_ref, line_ref, out_ref,
+    got, result, sent_in, got_in, own_in, sent_out, got_out, own_out,
+):
+    parts = lax.axis_size("vel")
+    blocks, planes, group, plane = cells_ref.shape
+    chunks = blocks // parts
+    me = lax.axis_index("vel")
+    mesh_ids = pl.DeviceIdType.MESH
+    peers = [lax.rem(me + n, parts) for n in range(parts)]
+    tables = (first_ref, second_ref, loss_ref, plane_ref, line_ref)
+
+    barrier = pltpu.get_barrier_semaphore()
+    for peer in peers[1:]:
+        pl.semaphore_signal(barrier, inc=1, device_id={"vel": peer}, device_id_type=mesh_ids)
+    pl.semaphore_wait(barrier, parts - 1)
+
+    def swap(chunk, from_ref, to_ref, send_sem, recv_sem, own_sem):
+        mine = chunk * parts + me
+        copies = []
+        for n, peer in enumerate(peers):
+            source = from_ref.at[chunk * parts + peer]
+            if n == 0:
+                copies.append(pltpu.make_async_copy(source, to_ref.at[mine], own_sem.at[chunk]))
+            else:
+                copies.append(
+                    pltpu.make_async_remote_copy(
+                        src_ref=source, dst_ref=to_ref.at[mine],
+                        send_sem=send_sem.at[chunk, n], recv_sem=recv_sem.at[chunk, n],
+                        device_id={"vel": peer}, device_id_type=mesh_ids,
+                    )
+                )
+            copies[-1].start()
+        return copies
+
+    incoming = [swap(chunk, cells_ref, got, sent_in, got_in, own_in) for chunk in range(chunks)]
+    outgoing = []
+    for chunk in range(chunks):
+        for copy in incoming[chunk][1:]:
+            copy.wait_recv()
+        incoming[chunk][0].wait()
+        held = slice(chunk * parts, (chunk + 1) * parts)
+        values = got[held].reshape(parts * planes * group, plane)
+        result[held] = collision(values, tables, parts * planes).reshape(parts, planes, group, plane)
+        outgoing.append(swap(chunk, result, out_ref, sent_out, got_out, own_out))
+    for copies in outgoing:
+        copies[0].wait()
+        for copy in copies[1:]:
+            copy.wait_recv()
+    for copies in incoming + outgoing:
+        for copy in copies[1:]:
+            copy.wait_send()
 
 
 def hartley_tables(vdim):
@@ -399,33 +458,54 @@
     return split(np.kron(table, table)), np.concatenate(split(np.kron(table, np.eye(GROUP))))
 
 
-def collide(cells, gain_first, gain_second, loss_rates):
+def collision_operands(gain_first, gain_second, loss_rates):
+    terms, plane = gain_first.shape[0], VDIM * VDIM
+    plane_table, line_table = hartley_tables(VDIM)
+    return (
+        gain_first.reshape(terms, VDIM, plane),
+        gain_second.reshape(terms, VDIM, plane),
+        loss_rates.reshape(VDIM, plane),
+        jnp.asarray(plane_table),
+        jnp.asarray(line_table),
+    )
+
+
+def collide(cells, operands):
     depth, count, plane = cells.shape
     spare = -count % GROUP
     if spare:
         cells = jnp.pad(cells, ((0, 0), (0, spare), (0, 0)))
-    terms = gain_first.shape[0]
-    plane_table, line_table = hartley_tables(VDIM)
     cell_spec = pl.BlockSpec((depth, GROUP, plane), lambda n: (0, n, 0))
 
     def whole(shape):
         return pl.BlockSpec(shape, lambda n: (0,) * len(shape))
 
-    multipliers = (
-        gain_first.reshape(terms, depth, plane),
-        gain_second.reshape(terms, depth, plane),
-        loss_rates.reshape(depth, plane),
-    )
-    tables = (jnp.asarray(plane_table), jnp.asarray(line_table))
     result = pl.pallas_call(
         collide_kernel,
         grid=((count + spare) // GROUP,),
-        in_specs=[cell_spec] + [whole(array.shape) for array in multipliers + tables],
+        in_specs=[cell_spec] + [whole(array.shape) for array in operands],
         out_specs=cell_spec,
         out_shape=jax.ShapeDtypeStruct(cells.shape, jnp.float32),
         compiler_params=pltpu.CompilerParams(vmem_limit_bytes=56 * 1024 * 1024),
-    )(cells, *multipliers, *tables)
+    )(cells, *operands)
     return result[:, :count]
+
+
+def swap_collide(cells, operands):
+    chunks, parts = cells.shape[0] // lax.axis_size("vel"), lax.axis_size("vel")
+    vmem = pl.BlockSpec(memory_space=pltpu.VMEM)
+    across = pltpu.SemaphoreType.DMA((chunks, parts))
+    own = pltpu.SemaphoreType.DMA((chunks,))
+    return pl.pallas_call(
+        swap_collide_kernel,
+        in_specs=[vmem] * (1 + len(operands)),
+        out_specs=vmem,
+        out_shape=jax.ShapeDtypeStruct(cells.shape, jnp.float32),
+        scratch_shapes=[pltpu.VMEM(cells.shape, jnp.float32)] * 2 + [across, across, own] * 2,
+        compiler_params=pltpu.CompilerParams(
+            collective_id=1, has_side_effects=True, vmem_limit_bytes=56 * 1024 * 1024
+        ),
+    )(cells, *operands)
 
 
 def shards(
@@ -451,20 +531,18 @@
     held = jnp.sum(collide_mask)[None]
 
     plane = VDIM * VDIM
-    if width % plane == 0:
-        planes, span = width // plane, plane
+    operands = collision_operands(gain_first, gain_second, loss_rates)
+    if width % plane == 0 and each % GROUP == 0:
+        sent = gather(chosen, section_two, (ACT // GROUP, width // plane, GROUP, plane))
+        change = swap_collide(sent, operands)
     else:
-        planes, span = 1, width
-    sent = gather(chosen, section_two, (parts, planes, each, span))
-    got = lax.all_to_all(sent, "vel", split_axis=0, concat_axis=0, tiled=True)
-    got = got.reshape(parts * planes, each, span)
-    if span != plane:
-        got = jnp.transpose(got, (1, 0, 2)).reshape(each, VDIM, plane).transpose(1, 0, 2)
-    change = collide(got, gain_first, gain_second, loss_rates)
-    if span != plane:
-        change = change.transpose(1, 0, 2).reshape(each, parts, span).transpose(1, 0, 2)
-    change = change.reshape(parts, planes, each, span)
-    change = lax.all_to_all(change, "vel", split_axis=0, concat_axis=0, tiled=True)
+        sent = gather(chosen, section_two, (parts, 1, each, width))
+        got = lax.all_to_all(sent, "vel", split_axis=0, concat_axis=0, tiled=True)
+        got = jnp.transpose(got.reshape(parts, each, width), (1, 0, 2))
+        got = got.reshape(each, VDIM, plane).transpose(1, 0, 2)
+        change = collide(got, operands).transpose(1, 0, 2).reshape(each, parts, width)
+        change = change.transpose(1, 0, 2)[:, None]
+        change = lax.all_to_all(change, "vel", split_axis=0, concat_axis=0, tiled=True)
     return scatter(chosen, held, section_two, change).reshape(blocks, cell_count, width)
 
 

time: 132 us -> 110 us (0.83)
  waiting for transfers between devices: 33 us -> 0 us
  Pallas kernels: 71.2 us -> 89.9 us
  starting transfers between devices: 9.34 us -> 0 us
    all_to_all x2 -> x0, waiting for transfers between devices: 33 us -> none  [the longest x1 19.8 us: shards(): lax.all_to_all(change, 'vel', split_axis=0, concat_axis=0, tiled=True)]
    pallas_call x1, Pallas kernels: 31.7 us -> 50.3 us  [swap_collide(): pl.pallas_call(swap_collide_kernel, in_specs=[vmem] * (1 + len(operands))...]
    all_to_all x2 -> x0, starting transfers between devices: 9.34 us -> none  [the longest x1 5.66 us: shards(): got = lax.all_to_all(sent, 'vel', split_axis=0, concat_axis=0, tiled=True)]
    reshape x3, local copies, waits for them, and re-layouts: 2.45 us -> 5.28 us  [the longest x1 1.88 us: collision_operands(): gain_first.reshape(terms, VDIM, plane)]
    unnamed x14 -> x4, local copies, waits for them, and re-layouts: 3.15 us -> 1.25 us
    pad x1, local copies, waits for them, and re-layouts: 2.85 us -> 1.37 us  [tiled(): rows = jnp.pad(rows, ((0, 0), (0, tiles * LANES - width)))]
  transfers between devices with their start and end apart: 2 -> 0, of which waited for: 2 -> 0; matrix products, arithmetic and copies ran while one was open for 2% -> 0% of each run, Pallas kernels for 0% -> 0%
where the time goes in v3:
time: 110 us; the launch traced here: 109 us
  Pallas kernels  89.9 us (82%)
  local copies, waits for them, and re-layouts  12.6 us (11%)
  other arithmetic  5.2 us (5%)
    pallas_call x1, Pallas kernels, swap_collide(): pl.pallas_call(swap_collide_kernel, in_specs=[vmem] * (1 + len(operands))...  50.3 us
    pallas_call x1, Pallas kernels, transport(): pl.pallas_call(transport_kernel, in_specs=[smem, smem, vmem, vmem], out_s...  30.7 us
    pallas_call x1, Pallas kernels, scatter(): pl.pallas_call(scatter_kernel, in_specs=[smem, smem, vmem, vmem], out_spe...  5.2 us
    pallas_call x1, Pallas kernels, gather(): pl.pallas_call(gather_kernel, in_specs=[pl.BlockSpec(memory_space=pltpu.S...  3.62 us
    reshape x1, local copies, waits for them, and re-layouts, shards(): scatter(chosen, held, section_two, change)  2.7 us

profile of v3, /device:TPU:1, one launch (start us, length us, event | category | flops | bytes accessed | tf_op | source)
XLA Modules:
  0.0 108.5 jit_solution(5308664450042445145)
XLA Ops:
  0.0 0.0 copy-start.1
  0.8 1.3 %reduce_sum.29 = s32[]{:T(128)} reduce(s32[256]{0:T(256)} %param.12, s32[]{:T(128)} %constant.49.clone.1), dimensions={0}, to_apply=%region_2.3 | reduce | flops 255 | bytes 1032 | tf_op jit(solution)/shard_map/reduce_sum | solution.py:531
  2.2 0.7 subtract_bitcast_fusion
  2.8 0.7 compare_bitcast_fusion
  3.5 0.7 broadcast_compare_fusion
  4.2 0.1 fusion.8
  4.2 0.1 reshape.159.source_ref
  4.3 0.8 select_reduce_fusion
  5.1 0.7 select_reduce_fusion.1.chosen_ref
  5.9 0.1 fusion.5
  6.0 0.1 compare_select_fusion
  6.1 0.1 stack.5
  6.2 1.5 %reshape.157.loss_ref = f32[24,576]{1,0:T(8,128)} reshape(f32[13824]{0:T(1024)} %param.15) | data formatting | bytes 110592 | tf_op jit(solution)/shard_map/reshape | solution.py:467
  7.7 1.9 %reshape.155.first_ref = f32[6,24,576]{2,1,0:T(8,128)} reshape(f32[6,13824]{1,0:T(8,128)} %param.13) | data formatting | bytes 663552 | tf_op jit(solution)/shard_map/reshape | solution.py:465
  9.6 1.9 %reshape.156.second_ref = f32[6,24,576]{2,1,0:T(8,128)} reshape(f32[6,13824]{1,0:T(8,128)} %param.14) | data formatting | bytes 663552 | tf_op jit(solution)/shard_map/reshape | solution.py:466
  11.5 0.0 copy-done.1
  11.5 1.4 %pad.8 = f32[256,1792]{0,1:T(8,128)} pad(f32[256,1728]{0,1:T(8,128)S(1)} %bitcast.16, f32[]{:T(128)} %constant.54.clone.1), padding=0_0x0_64 | pad | bytes 3604484 | tf_op jit(solution)/shard_map/jit(_pad)/pad | solution.py:278
  12.9 1.8 %copy.13 = f32[256,14,128]{2,0,1:T(8,128)S(1)} copy(f32[256,14,128]{0,2,1:T(8,128)} %bitcast.15) | data formatting | bytes 3670016 | tf_op jit(solution)/shard_map/reshape | solution.py:279
  14.7 30.7 %shard_map.91.cells_ref = f32[14,256,128]{2,1,0:T(8,128)S(1)} custom-call(f32[12]{0:T(128)S(1)} %reshape.159.source_ref, f32[1]{0:T(128)S(6)} %mul.6.ratio_ref, f32[14,256,128]{2,1,0:T(8,128)S(1)} %bitcast.13, f32[14,8,128]{2,1,0:T(8,128)S(1)} %pad_bitcast_fusion.speed_ref), custom_call_target="tpu_custom_call" | custom-call | tf_op jit(solution)/shard_map/pallas_call | solution.py:260
  45.4 0.0 copy-start
  45.4 1.2 %copy-done = f32[14,256,128]{2,1,0:T(8,128)} copy-done((f32[14,256,128]{2,1,0:T(8,128)}, f32[14,256,128]{2,1,0:T(8,128)S(1)}, u32[]{:S(2)}) %copy-start) | copy-done | bytes 1835032
  46.7 3.6 %shard_map.92.cells_ref = f32[16,3,8,576]{3,2,1,0:T(8,128)} custom-call(s32[128]{0:T(128)} %select_reduce_fusion.1.chosen_ref, f32[14,256,128]{2,1,0:T(8,128)} %copy-done), custom_call_target="tpu_custom_call" | custom-call | tf_op jit(solution)/shard_map/pallas_call | solution.py:305
  50.3 50.3 %shard_map.93.change_ref = f32[16,3,8,576]{3,2,1,0:T(8,128)} custom-call(f32[16,3,8,576]{3,2,1,0:T(8,128)} %shard_map.92.cells_ref, f32[6,24,576]{2,1,0:T(8,128)} %reshape.155.first_ref, f32[6,24,576]{2,1,0:T(8,128)} %reshape.156.second_ref, f32[24,576]{1,0:T(8,128)} %reshape.157.loss_ref, bf16[2,576,576]{2,1,0:T(8,128)(2,1)} %constant.63.clone.plane_ref, ...), custom_call_target="tpu_custom_call" | custom-call | tf_op jit(solution)/shard_map/pallas_call | solution.py:499
  100.6 5.2 %shard_map.94 = f32[256,1728]{1,0:T(8,128)} custom-call(s32[128]{0:T(128)} %select_reduce_fusion.1.chosen_ref, s32[1]{0:T(128)} %bitcast.count_ref, f32[14,256,128]{2,1,0:T(8,128)} %copy-done, f32[16,3,8,576]{3,2,1,0:T(8,128)} %shard_map.93.change_ref), custom_call_target="tpu_custom_call" | custom-call | tf_op jit(solution)/shard_map/pallas_call | solution.py:337
  105.8 2.7 %copy.14 = f32[1,256,1728]{1,2,0:T(8,128)} copy(f32[1,256,1728]{2,1,0:T(8,128)} %bitcast.14) | data formatting | bytes 3538944 | tf_op jit(solution)/shard_map/reshape | solution.py:546
  (2 shorter events, 0.0 us)
Async XLA Ops:
  0.0 11.5 %copy-start.1 = (f32[1,256,1728]{1,2,0:T(8,128)S(1)}, f32[1,256,1728]{1,2,0:T(8,128)}, u32[]{:S(2)}) copy-start(f32[1,256,1728]{1,2,0:T(8,128)} %param.9) | copy-start | bytes 5308420
  45.4 1.3 %copy-start = (f32[14,256,128]{2,1,0:T(8,128)}, f32[14,256,128]{2,1,0:T(8,128)S(1)}, u32[]{:S(2)}) copy-start(f32[14,256,128]{2,1,0:T(8,128)S(1)} %shard_map.91.cells_ref) | copy-start | bytes 5505028

commit v4 on v3

--- a/solution.py
+++ b/solution.py
@@ -393,6 +393,7 @@
 
 def swap_collide_kernel(
     cells_ref, first_ref, second_ref, loss_ref, plane_ref, line_ref, out_ref,
+    first_cube, second_cube, loss_cube,
     got, result, sent_in, got_in, own_in, sent_out, got_out, own_out,
 ):
     parts = lax.axis_size("vel")
@@ -401,7 +402,7 @@
     me = lax.axis_index("vel")
     mesh_ids = pl.DeviceIdType.MESH
     peers = [lax.rem(me + n, parts) for n in range(parts)]
-    tables = (first_ref, second_ref, loss_ref, plane_ref, line_ref)
+    tables = (first_cube, second_cube, loss_cube, plane_ref, line_ref)
 
     barrier = pltpu.get_barrier_semaphore()
     for peer in peers[1:]:
@@ -427,6 +428,12 @@
         return copies
 
     incoming = [swap(chunk, cells_ref, got, sent_in, got_in, own_in) for chunk in range(chunks)]
+    for row in range(parts * planes):
+        columns = slice(row * plane, (row + 1) * plane)
+        for term in range(first_ref.shape[0]):
+            first_cube[term, row : row + 1, :] = first_ref[term : term + 1, columns]
+            second_cube[term, row : row + 1, :] = second_ref[term : term + 1, columns]
+        loss_cube[row : row + 1, :] = loss_ref[:, columns]
     outgoing = []
     for chunk in range(chunks):
         for copy in incoming[chunk][1:]:
@@ -459,19 +466,15 @@
 
 
 def collision_operands(gain_first, gain_second, loss_rates):
-    terms, plane = gain_first.shape[0], VDIM * VDIM
     plane_table, line_table = hartley_tables(VDIM)
-    return (
-        gain_first.reshape(terms, VDIM, plane),
-        gain_second.reshape(terms, VDIM, plane),
-        loss_rates.reshape(VDIM, plane),
-        jnp.asarray(plane_table),
-        jnp.asarray(line_table),
-    )
+    return gain_first, gain_second, loss_rates[None], jnp.asarray(plane_table), jnp.asarray(line_table)
 
 
 def collide(cells, operands):
     depth, count, plane = cells.shape
+    gain_first, gain_second, loss_rates = operands[:3]
+    cube = (gain_first.shape[0], depth, plane)
+    operands = (gain_first.reshape(cube), gain_second.reshape(cube), loss_rates.reshape(cube[1:])) + operands[3:]
     spare = -count % GROUP
     if spare:
         cells = jnp.pad(cells, ((0, 0), (0, spare), (0, 0)))
@@ -496,12 +499,16 @@
     vmem = pl.BlockSpec(memory_space=pltpu.VMEM)
     across = pltpu.SemaphoreType.DMA((chunks, parts))
     own = pltpu.SemaphoreType.DMA((chunks,))
+    cube = (VDIM, cells.shape[3])
+    gains = pltpu.VMEM((operands[0].shape[0],) + cube, jnp.float32)
     return pl.pallas_call(
         swap_collide_kernel,
         in_specs=[vmem] * (1 + len(operands)),
         out_specs=vmem,
         out_shape=jax.ShapeDtypeStruct(cells.shape, jnp.float32),
-        scratch_shapes=[pltpu.VMEM(cells.shape, jnp.float32)] * 2 + [across, across, own] * 2,
+        scratch_shapes=[gains, gains, pltpu.VMEM(cube, jnp.float32)]
+        + [pltpu.VMEM(cells.shape, jnp.float32)] * 2
+        + [across, across, own] * 2,
         compiler_params=pltpu.CompilerParams(
             collective_id=1, has_side_effects=True, vmem_limit_bytes=56 * 1024 * 1024
         ),

time: 110 us -> 108 us (0.982)
  local copies, waits for them, and re-layouts: 12.6 us -> 10.2 us
    reshape x3 -> x0, local copies, waits for them, and re-layouts: 5.28 us -> none  [the longest x1 1.88 us: collision_operands(): gain_first.reshape(terms, VDIM, plane)]
    pad x1, local copies, waits for them, and re-layouts: 1.37 us -> 2.85 us  [tiled(): rows = jnp.pad(rows, ((0, 0), (0, tiles * LANES - width)))]
    broadcast_in_dim x0 -> x1, local copies, waits for them, and re-layouts: none -> 1.47 us  [collision_operands(): loss_rates[None]]
where the time goes in v4:
time: 108 us; the launch traced here: 106 us
  Pallas kernels  89.8 us (83%)
  local copies, waits for them, and re-layouts  10.2 us (9%)
  other arithmetic  5.2 us (5%)
    pallas_call x1, Pallas kernels, swap_collide(): pl.pallas_call(swap_collide_kernel, in_specs=[vmem] * (1 + len(operands))...  50.4 us
    pallas_call x1, Pallas kernels, transport(): pl.pallas_call(transport_kernel, in_specs=[smem, smem, vmem, vmem], out_s...  30.7 us
    pallas_call x1, Pallas kernels, scatter(): pl.pallas_call(scatter_kernel, in_specs=[smem, smem, vmem, vmem], out_spe...  5.08 us
    pallas_call x1, Pallas kernels, gather(): pl.pallas_call(gather_kernel, in_specs=[pl.BlockSpec(memory_space=pltpu.S...  3.62 us
    pad x1, local copies, waits for them, and re-layouts, tiled(): rows = jnp.pad(rows, ((0, 0), (0, tiles * LANES - width)))  2.85 us
    reshape x1, local copies, waits for them, and re-layouts, shards(): scatter(chosen, held, section_two, change)  2.7 us

profile of v4, /device:TPU:1, one launch (start us, length us, event | category | flops | bytes accessed | tf_op | source)
XLA Modules:
  0.0 106.0 jit_solution(9958064413084946315)
XLA Ops:
  0.7 1.3 %reduce_sum.29 = s32[]{:T(128)} reduce(s32[256]{0:T(256)} %param.12, s32[]{:T(128)} %constant.49.clone.1), dimensions={0}, to_apply=%region_2.3 | reduce | flops 255 | bytes 1032 | tf_op jit(solution)/shard_map/reduce_sum | solution.py:538
  2.0 0.7 subtract_bitcast_fusion
  2.7 0.7 compare_bitcast_fusion
  3.4 0.7 broadcast_compare_fusion
  4.0 0.1 fusion.8
  4.1 0.1 reshape.147.source_ref
  4.2 0.8 select_reduce_fusion
  5.0 0.7 select_reduce_fusion.1.chosen_ref
  5.7 0.1 fusion.5
  5.9 0.1 compare_select_fusion
  6.0 0.1 stack.5
  6.1 1.5 %broadcast_in_dim.54.loss_ref = f32[1,13824]{1,0:T(1,128)} reshape(f32[13824]{0:T(1024)} %param.15) | data formatting | bytes 110592 | tf_op jit(solution)/shard_map/broadcast_in_dim | solution.py:470
  7.6 2.8 %pad.8 = f32[256,1792]{0,1:T(8,128)} pad(f32[256,1728]{0,1:T(8,128)} %bitcast.16, f32[]{:T(128)} %constant.54.clone.1), padding=0_0x0_64 | pad | bytes 3604484 | tf_op jit(solution)/shard_map/jit(_pad)/pad | solution.py:278
  10.4 1.8 %copy.13 = f32[256,14,128]{2,0,1:T(8,128)S(1)} copy(f32[256,14,128]{0,2,1:T(8,128)} %bitcast.15) | data formatting | bytes 3670016 | tf_op jit(solution)/shard_map/reshape | solution.py:279
  12.2 30.7 %shard_map.91.cells_ref = f32[14,256,128]{2,1,0:T(8,128)S(1)} custom-call(f32[12]{0:T(128)S(1)} %reshape.147.source_ref, f32[1]{0:T(128)S(6)} %mul.6.ratio_ref, f32[14,256,128]{2,1,0:T(8,128)S(1)} %bitcast.13, f32[14,8,128]{2,1,0:T(8,128)S(1)} %pad_bitcast_fusion.speed_ref), custom_call_target="tpu_custom_call" | custom-call | tf_op jit(solution)/shard_map/pallas_call | solution.py:260
  42.9 0.0 copy-start
  43.0 1.2 %copy-done = f32[14,256,128]{2,1,0:T(8,128)} copy-done((f32[14,256,128]{2,1,0:T(8,128)}, f32[14,256,128]{2,1,0:T(8,128)S(1)}, u32[]{:S(2)}) %copy-start) | copy-done | bytes 1835032
  44.2 3.6 %shard_map.92.cells_ref = f32[16,3,8,576]{3,2,1,0:T(8,128)} custom-call(s32[128]{0:T(128)} %select_reduce_fusion.1.chosen_ref, f32[14,256,128]{2,1,0:T(8,128)} %copy-done), custom_call_target="tpu_custom_call" | custom-call | tf_op jit(solution)/shard_map/pallas_call | solution.py:305
  47.8 50.4 %shard_map.93.change_ref = f32[16,3,8,576]{3,2,1,0:T(8,128)} custom-call(f32[16,3,8,576]{3,2,1,0:T(8,128)} %shard_map.92.cells_ref, f32[6,13824]{1,0:T(8,128)} %first_ref.1, f32[6,13824]{1,0:T(8,128)} %second_ref.1, f32[1,13824]{1,0:T(1,128)} %broadcast_in_dim.54.loss_ref, bf16[2,576,576]{2,1,0:T(8,128)(2,1)} %constant.63.clone.plane_ref, ...), custom_call_target="tpu_custom_call" | custom-call | tf_op jit(solution)/shard_map/pallas_call | solution.py:504
  98.2 5.1 %shard_map.94 = f32[256,1728]{1,0:T(8,128)} custom-call(s32[128]{0:T(128)} %select_reduce_fusion.1.chosen_ref, s32[1]{0:T(128)} %bitcast.count_ref, f32[14,256,128]{2,1,0:T(8,128)} %copy-done, f32[16,3,8,576]{3,2,1,0:T(8,128)} %shard_map.93.change_ref), custom_call_target="tpu_custom_call" | custom-call | tf_op jit(solution)/shard_map/pallas_call | solution.py:337
  103.3 2.7 %copy.14 = f32[1,256,1728]{1,2,0:T(8,128)} copy(f32[1,256,1728]{2,1,0:T(8,128)} %bitcast.14) | data formatting | bytes 3538944 | tf_op jit(solution)/shard_map/reshape | solution.py:553
  (2 shorter events, 0.0 us)
Async XLA Ops:
  42.9 1.3 %copy-start = (f32[14,256,128]{2,1,0:T(8,128)}, f32[14,256,128]{2,1,0:T(8,128)S(1)}, u32[]{:S(2)}) copy-start(f32[14,256,128]{2,1,0:T(8,128)S(1)} %shard_map.91.cells_ref) | copy-start | bytes 5505028
